TPU v7x, 32 devices: a whole 2x2x4 slice. The times are simulated.
32 devices in a mesh: row: 16 (over z, x, core), col: 2 (over y).
Axes of the slice: x: 2, y: 2, z: 4, core: 2. Of those that a mesh axis runs over, the one named last changes fastest.
Arguments:
- embeddings: bfloat16 [16384, 768], P(('row', 'col')), may hold values from -7.5 to 7.5
- block_cluster: int32 [64], replicated, may hold values from 0 to 15, never falling along the last dimension, each value on 1 to 8 neighbouring positions
- partner_shift: int32 [16384], P(('row', 'col')), may hold values from 1 to 255
Outputs:
- item_loss: float32 [16384], P(('row', 'col'))
- embedding_grad: float32 [16384, 768], P(('row', 'col'))
Inputs may be any that keep to these rules, and one draw needn't show every extreme that they name: block_cluster never falls along the blocks; each value is held by 1 to 8 consecutive blocks, and some value by exactly 8.
All inputs are finite; a program needn't handle non-finite values.
Results may differ from a plain program's by a relative error of at most 0.0018.
Values may be sent and summed in bfloat16 or wider, within the bound.
A program may use at most 128 MiB of HBM per device.

v0:
```python
import functools

import jax
import jax.numpy as jnp
from jax import lax
from jax.experimental import pallas as pl
from jax.experimental.pallas import tpu as pltpu
from jax.sharding import PartitionSpec as P

BLOCK = 256
REACH = 4
CHUNK = 128
NEG = -1e30
F32 = jnp.float32


def kernel(
    row_axis, col_axis, devices, cols, scale,
    cluster_ref, e_ref, shift_ref,
    grad_ref, loss_ref,
    buf, scores, weights, top, total, lse_col, lse_send, lse_far, pos_score, qcol_ref, qrow_ref,
    recv, xs, ys, cs, zs, ls, lr,
):
    me = lax.axis_index(row_axis) * cols + lax.axis_index(col_axis)
    y = me % 2
    c = me // 2 % 2
    x = me // 4 % 2
    g = 2 * c + y
    gy = 2 * c + 1 - y
    gp = 2 * (1 - c) + y
    gpy = 2 * (1 - c) + 1 - y
    oth = 32 * (1 - x)
    adj = 32 * x
    xpeer = me + 4 - 8 * x
    ypeer = me + 1 - 2 * y
    cpeer = me + 2 - 4 * c
    zto = me + 8 - 16 * x
    zfrom = me - 8 + 16 * x
    z_send = (zto >= 0) & (zto < devices)
    z_recv = (zfrom >= 0) & (zfrom < devices)

    def at(device):
        return (device // cols, device % cols)

    def exists(device):
        return (device >= 0) & (device < devices)

    barrier = pltpu.get_barrier_semaphore()
    count = jnp.int32(0)
    for offset in (-8, -4, -3, -2, -1, 1, 2, 3, 4, 8):
        there = exists(me + offset)
        count = count + there.astype(jnp.int32)

        @pl.when(there)
        def _():
            pl.semaphore_signal(
                barrier, inc=1, device_id=at(me + offset), device_id_type=pl.DeviceIdType.MESH
            )
    pl.semaphore_wait(barrier, count)

    def rows(slot):
        return buf.at[pl.ds(pl.multiple_of(slot * CHUNK, CHUNK), CHUNK), :]

    def remote(src, slot, send, device):
        return pltpu.make_async_remote_copy(
            src_ref=src, dst_ref=rows(slot), send_sem=send, recv_sem=recv.at[slot],
            device_id=at(device), device_id_type=pl.DeviceIdType.MESH,
        )

    def own(i):
        return e_ref.at[pl.ds(i * CHUNK, CHUNK), :]

    def x_own(i):
        return remote(own(i), adj + 4 * g + i, xs.at[i], xpeer)

    def y_own(i):
        return remote(own(i), 16 + 4 * g + i, ys.at[i], ypeer)

    def c_own(i):
        return remote(own(i), 16 + 4 * g + i, cs.at[16 + 4 * g + i], cpeer)

    def x_relay(i):
        return remote(rows(16 + 4 * gy + i), adj + 4 * gy + i, xs.at[4 + i], xpeer)

    def y_relay(i):
        return remote(rows(oth + 4 * g + i), oth + 4 * g + i, ys.at[2 + i], ypeer)

    def z_need(r):
        return jnp.where(x == 0, r >= 4 * y + 2, r <= 4 * y + 9)

    def z_relay(r):
        return remote(rows(oth + r), adj + r, zs.at[r], zto)

    zy_send = z_recv & (c == 0) & (y == 1 - x)
    zy_skip = (c == 0) & (y == x)

    def z_gives(i):
        need = z_send & z_need(4 * gy + i)
        return need & ~zy_skip if i >= 2 else need

    def zy_relay(i):
        return remote(rows(adj + 4 * g + i), adj + 4 * g + i, ys.at[4 + i], ypeer)

    def c_relay(slot):
        return remote(rows(slot), slot, cs.at[slot], cpeer)

    def c_gives(slot):
        return (slot >= 4 * gp + 2) & (slot <= 4 * gp + 33)

    def c_takes(slot):
        return (slot >= 4 * g + 2) & (slot <= 4 * g + 33)

    def arrived(slot):
        remote(rows(slot), slot, zs.at[0], cpeer).wait_recv()

    def when(cond, action):
        pl.when(cond)(action)

    for i in range(2):
        x_own(2 + i).start()
        y_own(i).start()
    for i in range(4):
        c_own(i).start()

    when(~z_recv, lambda: buf.__setitem__(
        (pl.ds(pl.multiple_of(adj * CHUNK, CHUNK), 16 * CHUNK), slice(None)),
        jnp.zeros((16 * CHUNK, buf.shape[1]), buf.dtype)))
    for offset in (-4, -3, -2, -1, 1, 2, 3, 4):
        when(~exists(me + offset), lambda: lse_far.__setitem__(
            offset + 4, jnp.zeros(lse_far.shape[1:], F32)))

    n = e_ref.shape[0]
    blocks = cluster_ref.shape[0]

    def alive(k, r):
        there = 2 * me + k - 7
        near = jnp.maximum(jnp.minimum(there, blocks - 1), 0)
        same = cluster_ref[near] == cluster_ref[2 * me + r]
        return same & (there == near)

    place = lax.broadcasted_iota(jnp.int32, (1, n), 1)
    within = place % BLOCK
    goal = place - within + (within + shift_ref[...]) % BLOCK
    qrow_ref[...] = goal
    qcol_ref[...] = jnp.broadcast_to(goal.astype(F32), (128, n)).T[:, :1].astype(jnp.int32)

    half = lax.broadcasted_iota(jnp.int32, (n, BLOCK), 0)
    lane = lax.broadcasted_iota(jnp.int32, (n, BLOCK), 1)
    q = qcol_ref[...]
    own_scores = []
    for h in range(2):
        s = lax.dot_general(
            e_ref[...], e_ref[h * BLOCK:(h + 1) * BLOCK, :], (((1,), (1,)), ((), ())),
            preferred_element_type=F32) * scale
        cell = lane + h * BLOCK
        hit = jnp.sum(jnp.where(q == cell, s, 0.0), axis=1, keepdims=True)
        own_scores.append((s, hit))
        ok = jnp.concatenate(
            [jnp.full((BLOCK, BLOCK), alive(7 + h, r).astype(jnp.int32), jnp.int32) for r in range(2)], 0) > 0
        scores[7 + h] = jnp.where(ok & (half != cell), s, NEG)
    buf[pl.ds(pl.multiple_of((16 + 4 * g) * CHUNK, 4 * CHUNK), n), :] = e_ref[...]
    pos_score[...] = own_scores[0][1] + own_scores[1][1]
    m = jnp.maximum(jnp.max(scores[7], axis=1, keepdims=True), jnp.max(scores[8], axis=1, keepdims=True))
    top[...] = m
    total[...] = jnp.sum(jnp.exp(scores[7] - m), axis=1, keepdims=True) + jnp.sum(
        jnp.exp(scores[8] - m), axis=1, keepdims=True)

    def process(block):
        k = block - (2 * g + 1)

        @pl.when((k >= 0) & (k < 16))
        def _():
            far = buf[pl.ds(pl.multiple_of(block * BLOCK, BLOCK), BLOCK), :]
            for r in range(2):
                part = pl.ds(r * BLOCK, BLOCK)
                s = lax.dot_general(
                    e_ref[part, :], far, (((1,), (1,)), ((), ())),
                    preferred_element_type=F32) * scale
                s = jnp.where(alive(k, r), s, NEG)
                scores[k, part, :] = s
                old = top[part, :]
                new = jnp.maximum(old, jnp.max(s, axis=1, keepdims=True))
                total[part, :] = total[part, :] * jnp.exp(old - new) + jnp.sum(
                    jnp.exp(s - new), axis=1, keepdims=True)
                top[part, :] = new

    def give(slot, also=True):
        when(c_gives(slot) & also, lambda: c_relay(slot).start())

    def event(kind, i):
        if kind == "X":
            slot = oth + 4 * g + i
            arrived(slot)
            when(z_send & z_need(4 * g + i), lambda: z_relay(4 * g + i).start())
            if i >= 2:
                y_relay(i).start()
                y_own(i).start()
            give(slot)
        elif kind == "Y":
            slot = 16 + 4 * gy + i
            arrived(slot)
            if i < 2:
                x_relay(i).start()
                x_own(i).start()
            give(slot)
        elif kind == "D":
            slot = oth + 4 * gy + i
            arrived(slot)
            when(z_gives(i), lambda: z_relay(4 * gy + i).start())
            give(slot)
        else:
            e = 4 * (g if kind == "Z" else gy) + i

            def take():
                arrived(adj + e)
                if kind == "Z" and i >= 2:
                    when(zy_send, lambda: zy_relay(i).start())
                give(adj + e)
            when(z_recv & z_need(e), take)

    def c_wait(block, cond):
        for i in range(2):
            when(c_takes(2 * block + i) & cond, lambda: arrived(2 * block + i))

    def at_block(base, element, h):
        return base // 2 + 2 * element + h

    here = jnp.int32(16)
    steps = [
        ([("X", 2), ("Y", 0)], [(at_block(here, gp, 0), True), (at_block(here, gp, 1), True)]),
        ([("X", 3), ("Y", 1), ("Z", 2)], [(at_block(oth, g, 1), None), (at_block(here, gy, 0), None)]),
        ([("D", 0), ("D", 2), ("Z", 3)], [(at_block(oth, gp, 1), True), (at_block(here, gpy, 0), True)]),
        ([("X", 0), ("Y", 2), ("W", 0)], [(at_block(adj, g, 1), None), (at_block(adj, gp, 1), z_recv)]),
        ([("D", 1), ("D", 3), ("W", 2)], [(at_block(oth, gy, 0), None), (at_block(oth, gy, 1), None)]),
        ([("X", 1), ("Y", 3), ("Z", 0)], [(at_block(oth, g, 0), None), (at_block(here, gy, 1), None)]),
        ([("W", 1)], [(at_block(oth, gp, 0), True), (at_block(here, gpy, 1), True)]),
        ([("W", 3)], [(at_block(oth, gpy, 0), True), (at_block(oth, gpy, 1), True)]),
        ([], [(at_block(adj, gy, 0), None), (at_block(adj, gy, 1), None)]),
        ([], [(at_block(adj, gpy, 0), z_recv), (at_block(adj, gpy, 1), z_recv)]),
        ([("Z", 1)], [(at_block(adj, g, 0), None), (at_block(adj, gp, 0), z_recv)]),
    ]

    def step(u, carry):
        spots = [jnp.int32(0), jnp.int32(0)]
        for index, (events, ready) in enumerate(steps):
            for h in range(2):
                spots[h] = spots[h] + jnp.where(u == index, ready[h][0], 0)

            @pl.when(u == index)
            def _():
                for kind, i in events:
                    event(kind, i)
                for block, cond in ready:
                    if cond is not None:
                        c_wait(block, cond)
        for h in range(2):
            process(spots[h])
        return carry

    lax.fori_loop(0, len(steps), step, 0)

    lse = top[...] + jnp.log(total[...])
    lse_col[...] = lse
    loss = lse - pos_score[...]
    both = jnp.where(
        lax.broadcasted_iota(jnp.int32, (n, 128), 1) < 8,
        jnp.broadcast_to(lse, (n, 128)), jnp.broadcast_to(loss, (n, 128)))
    turned = both.T
    lse_send[...] = turned[:8, :]
    lse_far[4] = turned[:8, :]
    loss_ref[...] = turned[8]

    def lse_copy(offset):
        return pltpu.make_async_remote_copy(
            src_ref=lse_send, dst_ref=lse_far.at[4 - offset],
            send_sem=ls.at[4 + offset], recv_sem=lr.at[4 - offset],
            device_id=at(me + offset), device_id_type=pl.DeviceIdType.MESH,
        )

    for offset in (-4, 4, -3, 3, -2, 2, -1, 1):
        when(exists(me + offset), lambda: lse_copy(offset).start())

    def fill(k):
        offset = (k - 7) // 2
        h = (k - 7) % 2
        s = scores[k]
        w = jnp.exp(s - lse_col[...]) + jnp.exp(
            s - lse_far[offset + 4][0:1, h * BLOCK:(h + 1) * BLOCK])
        if offset == 0:
            cell = lax.broadcasted_iota(jnp.int32, (n, BLOCK), 1) + h * BLOCK
            line = lax.broadcasted_iota(jnp.int32, (n, BLOCK), 0)
            w = w - (qcol_ref[...] == cell).astype(F32)
            w = w - (qrow_ref[0:1, h * BLOCK:(h + 1) * BLOCK] == line).astype(F32)
        weights[:, k * BLOCK:(k + 1) * BLOCK] = w.astype(jnp.bfloat16)

    width = e_ref.shape[1]

    def part_of(first, many, columns):
        near = buf[pl.ds(pl.multiple_of((2 * g + 1 + first) * BLOCK, BLOCK), many * BLOCK), columns]
        left = weights[:, first * BLOCK:(first + many) * BLOCK]
        return jnp.dot(left, near, preferred_element_type=F32)

    def own_product(t, carry):
        columns = pl.ds(pl.multiple_of(t * 256, 256), 256)
        grad_ref[:, columns] = part_of(7, 2, columns)
        return carry

    def rest_product(t, carry):
        columns = pl.ds(pl.multiple_of(t * 256, 256), 256)
        rest = part_of(0, 7, columns) + part_of(9, 7, columns)
        grad_ref[:, columns] = (grad_ref[:, columns] + rest) * scale
        return carry

    fill(7)
    fill(8)
    lax.fori_loop(0, width // 256, own_product, 0)
    for offset in (-1, 1, -2, 2, -3, 3, -4, 4):
        when(exists(me + offset), lambda: lse_copy(-offset).wait_recv())
        for k in range(16):
            if (k - 7) // 2 == offset:
                fill(k)
    lax.fori_loop(0, width // 256, rest_product, 0)

    for offset in (-4, 4, -3, 3, -2, 2, -1, 1):
        when(exists(me + offset), lambda: lse_copy(offset).wait_send())
    for i in range(4):
        x_own(i).wait_send()
        y_own(i).wait_send()
        c_own(i).wait_send()
        when(z_send & z_need(4 * g + i), lambda: z_relay(4 * g + i).wait_send())
        when(z_gives(i), lambda: z_relay(4 * gy + i).wait_send())
        for slot in (oth + 4 * g + i, 16 + 4 * gy + i, oth + 4 * gy + i):
            when(c_gives(slot), lambda: c_relay(slot).wait_send())
        for e in (4 * g + i, 4 * gy + i):
            when(c_gives(adj + e) & z_recv & z_need(e), lambda: c_relay(adj + e).wait_send())
        if i < 2:
            x_relay(i).wait_send()
        else:
            y_relay(i).wait_send()
            when(zy_send, lambda: zy_relay(i).wait_send())


def solution(mesh):
    row_axis, col_axis = mesh.axis_names
    devices = mesh.shape[row_axis] * mesh.shape[col_axis]
    cols = mesh.shape[col_axis]

    def shards(embeddings, block_cluster, partner_shift):
        rows, width = embeddings.shape
        vmem = pl.BlockSpec(memory_space=pltpu.VMEM)
        grad, loss = pl.pallas_call(
            functools.partial(kernel, row_axis, col_axis, devices, cols, width ** (-0.5)),
            out_shape=(
                jax.ShapeDtypeStruct((rows, width), F32),
                jax.ShapeDtypeStruct((rows,), F32),
            ),
            in_specs=[pl.BlockSpec(memory_space=pltpu.SMEM), vmem, vmem],
            out_specs=(vmem, vmem),
            scratch_shapes=[
                pltpu.VMEM((24 * BLOCK, width), jnp.bfloat16),
                pltpu.VMEM((16, rows, BLOCK), F32),
                pltpu.VMEM((rows, 16 * BLOCK), jnp.bfloat16),
                pltpu.VMEM((rows, 1), F32),
                pltpu.VMEM((rows, 1), F32),
                pltpu.VMEM((rows, 1), F32),
                pltpu.VMEM((8, rows), F32),
                pltpu.VMEM((2 * REACH + 1, 8, rows), F32),
                pltpu.VMEM((rows, 1), F32),
                pltpu.VMEM((rows, 1), jnp.int32),
                pltpu.VMEM((1, rows), jnp.int32),
                pltpu.SemaphoreType.DMA((48,)),
                pltpu.SemaphoreType.DMA((6,)),
                pltpu.SemaphoreType.DMA((8,)),
                pltpu.SemaphoreType.DMA((48,)),
                pltpu.SemaphoreType.DMA((16,)),
                pltpu.SemaphoreType.DMA((2 * REACH + 1,)),
                pltpu.SemaphoreType.DMA((2 * REACH + 1,)),
            ],
            compiler_params=pltpu.CompilerParams(
                collective_id=0, has_side_effects=True, vmem_limit_bytes=34 * 1024 * 1024
            ),
        )(block_cluster, embeddings, partner_shift.reshape(1, rows))
        return loss, grad

    in_specs = (P((row_axis, col_axis), None), P(), P((row_axis, col_axis)))
    out_specs = (P((row_axis, col_axis)), P((row_axis, col_axis), None))
    return jax.shard_map(shards, mesh=mesh, in_specs=in_specs, out_specs=out_specs, check_vma=False)
```

profile of v0, /device:TPU:16, one launch (start us, length us, event | category | flops | bytes accessed | tf_op | source)
XLA Modules:
  0.0 58.0 jit_solution(792214164556928657)
XLA Ops:
  0.6 0.0 copy-start
  0.6 1.1 %copy-done = bf16[512,768]{1,0:T(8,128)(2,1)S(1)} copy-done((bf16[512,768]{1,0:T(8,128)(2,1)S(1)}, bf16[512,768]{1,0:T(8,128)(2,1)}, u32[]{:S(2)}) %copy-start) | copy-done | bytes 786456
  1.8 0.0 copy-start.1
  1.8 0.7 %copy-done.1 = s32[512]{0:T(512)S(1)} copy-done((s32[512]{0:T(512)S(1)}, s32[512]{0:T(512)}, u32[]{:S(2)}) %copy-start.1) | copy-done | bytes 2072
  2.4 0.0 copy-start.2
  2.4 0.7 %copy-done.2 = s32[64]{0:T(128)S(1)} copy-done((s32[64]{0:T(128)S(1)}, s32[64]{0:T(128)}, u32[]{:S(2)}) %copy-start.2) | copy-done | bytes 280
  3.1 53.1 %shard_map.50 = (f32[512,768]{1,0:T(8,128)S(1)}, f32[512]{0:T(512)S(1)}) custom-call(s32[64]{0:T(128)S(1)} %copy-done.2, bf16[512,768]{1,0:T(8,128)(2,1)S(1)} %copy-done, s32[1,512]{1,0:T(1,128)S(1)} %bitcast.1), custom_call_target="tpu_custom_call" | custom-call | tf_op jit(solution)/shard_map/pallas_call | solution.py:351
  56.2 0.6 %copy.7 = f32[512]{0:T(512)} copy(f32[512]{0:T(512)S(1)} %get-tuple-element.8) | data formatting | bytes 4096
  56.8 1.1 %copy.8 = f32[512,768]{1,0:T(8,128)} copy(f32[512,768]{1,0:T(8,128)S(1)} %get-tuple-element.9) | data formatting | bytes 3145728
Async XLA Ops:
  0.6 1.1 %copy-start = (bf16[512,768]{1,0:T(8,128)(2,1)S(1)}, bf16[512,768]{1,0:T(8,128)(2,1)}, u32[]{:S(2)}) copy-start(bf16[512,768]{1,0:T(8,128)(2,1)} %e_ref.1) | copy-start | bytes 2359300
  1.8 0.7 %copy-start.1 = (s32[512]{0:T(512)S(1)}, s32[512]{0:T(512)}, u32[]{:S(2)}) copy-start(s32[512]{0:T(512)} %param.5) | copy-start | bytes 6148
  2.4 0.7 %copy-start.2 = (s32[64]{0:T(128)S(1)}, s32[64]{0:T(128)}, u32[]{:S(2)}) copy-start(s32[64]{0:T(128)} %cluster_ref.1) | copy-start | bytes 772
where the time goes:
time: 58.2 us; the launch traced here: 58 us
  Pallas kernels  53.1 us (91%)
  local copies, waits for them, and re-layouts  4.18 us (7%)
  between operations  0.65 us (1%)
    pallas_call x1, Pallas kernels, shards(): pl.pallas_call(functools.partial(kernel, row_axis, col_axis, devices, col...  53.1 us
    unnamed x8, local copies, waits for them, and re-layouts  4.18 us

commit v1 on v0

v1 whole, which is shorter than its diff:
```python
import functools

import jax
import jax.numpy as jnp
from jax import lax
from jax.experimental import pallas as pl
from jax.experimental.pallas import tpu as pltpu
from jax.sharding import PartitionSpec as P

BLOCK = 256
MOST = 8
REACH = 4
CHUNK = 128
HALF = 64
NEG = -1e30
F32 = jnp.float32
MESH = pl.DeviceIdType.MESH

X_IN = (
    (40, 41, 34, 35, 36, 37, 38, 39, 32, 33, 10, 11),
    (38, 44, 39, 45, 43, 42, 14, 15, 33, 32, 37, 36),
)
Y_IN = (
    (20, 21, 30, 31, 22, 23, 28, 29, 12, 13, 14, 15),
    (27, 26, 25, 24, 40, 41, 16, 17, 18, 19, 34, 35),
)
Z_IN = (
    (8, 9, 2, 3, 4, 5, 6, 7),
    (6, 12, 7, 13, 8, 11, 9, 10),
)
BACK = ((17, 16), (21, 20))
OWN = (((16, 17, 18, 19), (24, 25, 26, 27)), ((20, 21, 22, 23), (28, 29, 30, 31)))
SCORE = (
    (
        {0: (12, 13), 2: (10,), 4: (4, 15), 6: (1, 11), 8: (2, 14), 10: (3, 16), 11: (6,), 12: (5, 7)},
        {0: (8, 9), 2: (20, 10), 4: (17, 15), 6: (18, 11), 8: (19, 14), 10: (16, 6), 12: (5, 7)},
    ),
    (
        {0: (14, 15), 2: (13,), 4: (12,), 5: (3,), 6: (6,), 8: (7, 8), 9: (4,), 10: (5, 9), 11: (16,), 12: (17, 18)},
        {0: (10, 11), 2: (13,), 3: (19,), 4: (12, 22), 6: (20, 21), 8: (7, 8), 10: (9, 16), 12: (17, 18)},
    ),
)
STEPS = 13


def events_of(t):
    x_out = [("T", s - (14 if t == 0 else 10)) if s < 16 else ("S", 63 - s) for s in X_IN[1 - t]]
    y_out = [("S", s) for s in Y_IN[1 - t]]
    z_out = [("S", s + 32) for s in Z_IN[t]]
    lists = {"X": x_out, "Y": y_out, "Z": z_out}
    ahead = {"X": 0, "Y": 0, "Z": 0}
    have = {("S", s) for c in range(2) for s in OWN[t][c]}

    def ready():
        out = []
        for link, items in lists.items():
            while ahead[link] < len(items) and items[ahead[link]] in have:
                out.append((link, ahead[link]))
                ahead[link] += 1
        return out

    first = ready()
    steps = []
    for u in range(STEPS):
        now = []
        if u < 12:
            now += [("X", u, ("S", X_IN[t][u])), ("Y", u, ("S", Y_IN[t][u]))]
        if u < 2:
            now.append(("T", u, ("T", u)))
        if 2 <= u < 10:
            now.append(("Z", u - 2, ("S", Z_IN[t][u - 2])))
        done = []
        for kind, i, item in now:
            have.add(item)
            done.append((kind, i, ready()))
        steps.append(done)
    assert all(ahead[link] == len(items) for link, items in lists.items())
    return lists, first, steps


def kernel(
    row_axis, col_axis, devices, cols, scale,
    cluster_hbm, e_hbm, shift_hbm,
    grad_ref, loss_ref,
    buf, thru, scores, first_exp, weights, top, total, lse_col, lse_send, lse_far, pos_score, qcol_ref, qrow_ref,
    cluster_ref, shift_ref,
    recv, trecv, xs, ys, zs, bs, cs, ls, lr, own_sem,
):
    me = lax.axis_index(row_axis) * cols + lax.axis_index(col_axis)
    y = me % 2
    c = me // 2 % 2
    x = me // 4 % 2
    g = 2 * c + y
    yt = (x + y) % 2
    ct = (x + c) % 2
    xpeer = me + 4 - 8 * x
    ypeer = me + 1 - 2 * y
    cpeer = me + 2 - 4 * c
    zto = me + 8 - 16 * x
    zfrom = me - 8 + 16 * x
    z_send = (zto >= 0) & (zto < devices)
    z_recv = (zfrom >= 0) & (zfrom < devices)

    def at(device):
        return (device // cols, device % cols)

    def exists(device):
        return (device >= 0) & (device < devices)

    def when(cond, action):
        if cond is True:
            action()
        else:
            pl.when(cond)(action)

    def both(*conds):
        conds = [cond for cond in conds if cond is not True]
        return functools.reduce(lambda a, b: a & b, conds) if conds else True

    barrier = pltpu.get_barrier_semaphore()
    count = jnp.int32(0)
    for there, device in ((True, xpeer), (True, ypeer), (True, cpeer), (z_send, zto), (z_recv, zfrom)):
        when(there, lambda: pl.semaphore_signal(barrier, inc=1, device_id=at(device), device_id_type=MESH))
        count = count + (1 if there is True else there.astype(jnp.int32))
    pl.semaphore_wait(barrier, count)

    n = e_hbm.shape[0]
    first = 8 + 2 * g

    def slot_of(s):
        return s + x * (47 - 2 * s)

    def rows(slot, half):
        return buf.at[slot // 2, pl.ds(pl.multiple_of(slot % 2 * CHUNK + half * HALF, HALF), HALF), :]

    def copy(src, dst, send, receive, device):
        return pltpu.make_async_remote_copy(
            src_ref=src, dst_ref=dst, send_sem=send, recv_sem=receive,
            device_id=at(device), device_id_type=MESH,
        )

    def arrived(slot, half):
        copy(rows(slot, half), rows(slot, half), cs.at[0], recv.at[2 * slot + half], cpeer).wait_recv()

    def mine(s):
        return e_hbm.at[pl.ds(pl.multiple_of((slot_of(s) - 16 - 4 * g) * CHUNK + c * HALF, HALF), HALF), :]

    def source(t, item, own=False):
        kind, s = item
        if kind == "T":
            return thru.at[pl.ds(s * HALF, HALF), :]
        return mine(s) if own else rows(slot_of(s), c)

    def link_copy(t, lists, link, i, own=False):
        item = lists[link][i]
        src = source(t, item, own)
        if link == "X":
            s = X_IN[1 - t][i]
            slot = s + (1 - x) * (47 - 2 * s)
            return copy(src, rows(slot, c), xs.at[i], recv.at[2 * slot + c], xpeer)
        if link == "Y":
            slot = slot_of(Y_IN[1 - t][i])
            return copy(src, rows(slot, c), ys.at[i], recv.at[2 * slot + c], ypeer)
        slot = slot_of(Z_IN[t][i])
        return copy(src, rows(slot, c), zs.at[i], recv.at[2 * slot + c], zto)

    def link_cond(t, link, i):
        if link == "Z":
            return z_send
        if link == "X":
            return z_send if X_IN[1 - t][i] < 16 else True
        return z_recv if Y_IN[1 - t][i] < 16 else True

    def back_copy(t, i, own=False):
        src = source(t, ("S", BACK[t][i]), own)
        return copy(src, thru.at[pl.ds(i * HALF, HALF), :], bs.at[i], trecv.at[i], zfrom)

    def own_half(i, half):
        return e_hbm.at[pl.ds(i * CHUNK + half * HALF, HALF), :]

    def c_own(i, half, j):
        slot = 16 + 4 * g + i
        return copy(own_half(i, half), rows(slot, half), cs.at[32 + j], recv.at[2 * slot + half], cpeer)

    def c_copy(s, j):
        slot = slot_of(s)
        return copy(rows(slot, c), rows(slot, c), cs.at[j], recv.at[2 * slot + c], cpeer)

    def c_cond(t, s):
        low = [8 * k + 4 * t + 2 <= s <= 8 * k + 4 * t + 33 for k in range(2)]
        if low[0] and low[1]:
            need = True
        elif low[0]:
            need = ct == 1
        elif low[1]:
            need = ct == 0
        else:
            return False
        return both(need, z_recv if s < 16 else True)

    def c_all(t):
        places = [(s, j) for j, s in enumerate(X_IN[t] + Y_IN[t] + Z_IN[t])]
        return [(s, j, c_cond(t, s)) for s, j in places if c_cond(t, s) is not False]

    plans = [events_of(t) for t in range(2)]

    own_copies = [
        pltpu.make_async_copy(e_hbm.at[pl.ds(h * BLOCK, BLOCK), :], buf.at[first + h], own_sem.at[3 * h]) for h in range(2)]
    cluster_copy = pltpu.make_async_copy(cluster_hbm, cluster_ref, own_sem.at[1])
    shift_copy = pltpu.make_async_copy(shift_hbm, shift_ref, own_sem.at[2])
    for t in range(2):
        for k in range(2):
            @pl.when((yt == t) & (ct == k))
            def _():
                lists, first, _ = plans[t]
                opening = [(link, i) for link, i in first] + [("B", i) for i in range(2)]

                def slot_at(link, i):
                    return BACK[t][i] if link == "B" else lists[link][i][1]

                def send(link, i, own):
                    if link == "B":
                        when(z_recv, lambda: back_copy(t, i, own).start())
                    else:
                        when(link_cond(t, link, i), lambda: link_copy(t, lists, link, i, own).start())

                started = {"X": 0, "Y": 0, "B": 0}
                queue = {link: [i for name, i in opening if name == link] for link in ("X", "Y", "B")}
                plan = {}
                for link, items in queue.items():
                    mine_, other = ([i for i in items if (slot_at(link, i) in OWN[t][k]) == flag] for flag in (True, False))
                    order = []
                    for spot in range(len(items)):
                        take = mine_ if (spot == 0 and mine_) or not other or (mine_ and mine_[0] < other[0]) else other
                        order.append(take.pop(0))
                    plan[link] = order
                leads = []
                for link in ("Y", "X", "B"):
                    while plan[link] and slot_at(link, plan[link][0]) in OWN[t][k]:
                        leads.append((link, plan[link].pop(0)))
                for link, i in leads[:2]:
                    send(link, i, True)
                uses = []
                for link in ("Y", "X", "B", "Y", "X", "B", "Y", "X", "B", "Y", "X", "B", "Y", "Y", "Y", "Y", "X", "X"):
                    if plan[link]:
                        uses.append((link, plan[link].pop(0)))
                assert not any(plan.values())
                order = []
                for s in [s for link, i in [*leads, *uses] for s in [slot_at(link, i)]] + list(OWN[t][k]):
                    if s in OWN[t][k] and s not in order:
                        order.append(s)
                for j, s in enumerate(order):
                    i = slot_of(s) - 16 - 4 * g
                    copy(
                        e_hbm.at[pl.ds(pl.multiple_of(i * CHUNK + (1 - c) * HALF, HALF), HALF), :],
                        rows(slot_of(s), 1 - c), cs.at[32 + j], recv.at[2 * slot_of(s) + 1 - c], cpeer).start()
                for link, i in leads[2:]:
                    send(link, i, True)
                for own_copy in own_copies:
                    own_copy.start()
                cluster_copy.start()
                shift_copy.start()
                for j, s in enumerate(order):
                    copy(mine(s), rows(slot_of(s), c), cs.at[36 + j], recv.at[2 * slot_of(s) + c], cpeer).start()
                waited = set()
                for link, i in uses:
                    s = slot_at(link, i)
                    if s in OWN[t][k]:
                        send(link, i, True)
                        continue
                    if s not in waited:
                        waited.add(s)
                        arrived(slot_of(s), c)
                    send(link, i, False)
                for s in OWN[t][1 - k]:
                    if s not in waited:
                        arrived(slot_of(s), c)

    adj = 32 * x
    when(~z_recv, lambda: buf.__setitem__(
        pl.ds(adj // 2, 8), jnp.zeros((8, *buf.shape[1:]), buf.dtype)))
    for offset in (-4, -3, -2, -1, 1, 2, 3, 4):
        when(~exists(me + offset), lambda: lse_far.__setitem__(
            pl.ds(2 * (offset + REACH), 2), jnp.zeros((2, *lse_far.shape[1:]), F32)))

    blocks = cluster_ref.shape[0]
    cluster_copy.wait()
    shift_copy.wait()

    def alive(k, r):
        there = 2 * me + k - 7
        near = jnp.maximum(jnp.minimum(there, blocks - 1), 0)
        same = cluster_ref[near] == cluster_ref[2 * me + r]
        return same & (there == near)

    place = lax.broadcasted_iota(jnp.int32, (1, n), 1)
    within = place % BLOCK
    goal = place - within + (within + shift_ref[...]) % BLOCK
    qrow_ref[...] = goal
    qcol_ref[...] = jnp.broadcast_to(goal.astype(F32), (128, n)).T[:, :1].astype(jnp.int32)

    for own_copy in own_copies:
        own_copy.wait()
    half = lax.broadcasted_iota(jnp.int32, (n, BLOCK), 0)
    lane = lax.broadcasted_iota(jnp.int32, (n, BLOCK), 1)
    q = qcol_ref[...]
    own_scores = []
    for h in range(2):
        s = lax.dot_general(
            buf[pl.ds(first, 2)].reshape(n, -1), buf[first + h], (((1,), (1,)), ((), ())),
            preferred_element_type=F32) * scale
        cell = lane + h * BLOCK
        hit = jnp.sum(jnp.where(q == cell, s, 0.0), axis=1, keepdims=True)
        own_scores.append(hit)
        ok = jnp.concatenate(
            [jnp.full((BLOCK, BLOCK), alive(7 + h, r).astype(jnp.int32), jnp.int32) for r in range(2)], 0) > 0
        scores[7 + h] = jnp.where(ok & (half != cell), s, NEG)
    pos_score[...] = own_scores[0] + own_scores[1]
    m = jnp.maximum(jnp.max(scores[7], axis=1, keepdims=True), jnp.max(scores[8], axis=1, keepdims=True))
    top[...] = m
    total[...] = jnp.sum(jnp.exp(scores[7] - m), axis=1, keepdims=True) + jnp.sum(
        jnp.exp(scores[8] - m), axis=1, keepdims=True)

    def process(block):
        k = block - (2 * g + 1)

        @pl.when((k >= 0) & (k < 16))
        def _():
            far = buf[block]
            for r in range(2):
                part = pl.ds(r * BLOCK, BLOCK)
                s = lax.dot_general(
                    buf[first + r], far,
                    (((1,), (1,)), ((), ())), preferred_element_type=F32) * scale
                s = jnp.where(alive(k, r), s, NEG)
                scores[k, part, :] = s
                old = top[part, :]
                new = jnp.maximum(old, jnp.max(s, axis=1, keepdims=True))
                total[part, :] = total[part, :] * jnp.exp(old - new) + jnp.sum(
                    jnp.exp(s - new), axis=1, keepdims=True)
                top[part, :] = new

    def event(t, kind, i, sends):
        lists = plans[t][0]

        def run():
            if kind == "T":
                when(z_send, lambda: copy(
                    thru.at[pl.ds(i * HALF, HALF), :], thru.at[pl.ds(i * HALF, HALF), :],
                    bs.at[i], trecv.at[i], zto).wait_recv())
            else:
                s = {"X": X_IN, "Y": Y_IN, "Z": Z_IN}[kind][t][i]
                when(z_recv if s < 16 else True, lambda: arrived(slot_of(s), c))
            for link, j in sends:
                when(link_cond(t, link, j), lambda: link_copy(t, lists, link, j, False).start())
            if kind != "T":
                need = c_cond(t, s)
                if need is not False:
                    j = i + {"X": 0, "Y": 12, "Z": 24}[kind]
                    when(need, lambda: c_copy(s, j).start())
        run()

    def step(u, carry):
        spots = [jnp.int32(-1), jnp.int32(-1)]
        for index in range(STEPS):
            for t in range(2):
                for k in range(2):
                    here = (u == index) & (yt == t) & (ct == k)
                    for h, block in enumerate(SCORE[t][k].get(index, ())):
                        spots[h] = jnp.where(here, block + x * (23 - 2 * block), spots[h])
                here = (u == index) & (yt == t)

                @pl.when(here)
                def _():
                    for kind, i, sends in plans[t][2][index]:
                        event(t, kind, i, sends)
                    for k in range(2):
                        blocks_now = SCORE[t][k].get(index, ())
                        if blocks_now:
                            @pl.when(ct == k)
                            def _():
                                for block in blocks_now:
                                    for s in (2 * block, 2 * block + 1):
                                        when(z_recv if s < 16 else True, lambda: arrived(slot_of(s), 1 - c))
        for h in range(2):
            process(spots[h])
        return carry

    lax.fori_loop(0, STEPS, step, 0)

    lse = top[...] + jnp.log(total[...])
    lse_col[...] = lse
    loss = lse - pos_score[...]
    pair = jnp.where(
        lax.broadcasted_iota(jnp.int32, (n, 128), 1) < 8,
        jnp.broadcast_to(lse, (n, 128)), jnp.broadcast_to(loss, (n, 128)))
    turned = pair.T
    for h in range(2):
        row = turned[:1, h * BLOCK:(h + 1) * BLOCK]
        lse_send[h] = row
        lse_far[2 * REACH + h] = row
    loss_ref[...] = turned[8]

    def lse_copy(offset):
        return copy(
            lse_send, lse_far.at[pl.ds(2 * (REACH - offset), 2)], ls.at[REACH + offset], lr.at[REACH - offset],
            me + offset)

    for offset in (-4, 4, -3, 3, -2, 2, -1, 1):
        when(exists(me + offset), lambda: lse_copy(offset).start())

    lows = []
    for r in range(2):
        low = jnp.int32(r)
        for k in range(r, 7 + r):
            low = low + jnp.where(alive(k, r), 0, 1)
        lows.append(low)

    for h in range(2):
        s = scores[7 + h]
        w = jnp.exp(s - lse_col[...]) + jnp.exp(s - lse_far[2 * REACH + h])
        cell = lax.broadcasted_iota(jnp.int32, (n, BLOCK), 1) + h * BLOCK
        line = lax.broadcasted_iota(jnp.int32, (n, BLOCK), 0)
        w = w - (qcol_ref[...] == cell).astype(F32)
        w = w - (qrow_ref[0:1, h * BLOCK:(h + 1) * BLOCK] == line).astype(F32)
        weights[:, h * BLOCK:(h + 1) * BLOCK] = w.astype(jnp.bfloat16)
        scores[7 + h] = jnp.full((n, BLOCK), NEG, F32)

    width = e_hbm.shape[1]

    def own_product(t, carry):
        columns = pl.ds(pl.multiple_of(t * 256, 256), 256)
        grad_ref[:, columns] = jnp.dot(
            weights[:, :2 * BLOCK], buf[pl.ds(first, 2), :, columns].reshape(n, -1), preferred_element_type=F32)
        return carry

    lax.fori_loop(0, width // 256, own_product, 0)

    for r in range(2):
        part = pl.ds(r * BLOCK, BLOCK)
        for j in range(MOST):
            first_exp[part, j * BLOCK:(j + 1) * BLOCK] = jnp.exp(scores[lows[r] + j, part, :] - lse_col[part, :])

    for offset in (-1, 1, -2, 2, -3, 3, -4, 4):
        when(exists(me + offset), lambda: lse_copy(-offset).wait_recv())
    for r in range(2):
        part = pl.ds(r * BLOCK, BLOCK)
        for j in range(MOST):
            k = lows[r] + j
            w = first_exp[part, j * BLOCK:(j + 1) * BLOCK] + jnp.exp(scores[k, part, :] - lse_far[k + 1])
            weights[part, j * BLOCK:(j + 1) * BLOCK] = w.astype(jnp.bfloat16)

    for t in range(width // 256):
        columns = pl.ds(t * 256, 256)
        for r in range(2):
            part = pl.ds(r * BLOCK, BLOCK)
            near = jnp.concatenate([buf[2 * g + 1 + lows[r] + j, :, columns] for j in range(MOST)], 0)
            rest = jnp.dot(weights[part, :], near, preferred_element_type=F32)
            grad_ref[part, columns] = (grad_ref[part, columns] + rest) * scale

    for offset in (-4, 4, -3, 3, -2, 2, -1, 1):
        when(exists(me + offset), lambda: lse_copy(offset).wait_send())
    for t in range(2):
        @pl.when(yt == t)
        def _():
            lists = plans[t][0]
            for link, items in lists.items():
                for i in range(len(items)):
                    when(link_cond(t, link, i), lambda: link_copy(t, lists, link, i, False).wait_send())
            for s, j, need in c_all(t):
                when(need, lambda: c_copy(s, j).wait_send())
            for i in range(2):
                when(z_recv, lambda: back_copy(t, i, False).wait_send())
    for j in range(8):
        copy(rows(16, 0), rows(16, 0), cs.at[32 + j], recv.at[0], cpeer).wait_send()


def solution(mesh):
    row_axis, col_axis = mesh.axis_names
    devices = mesh.shape[row_axis] * mesh.shape[col_axis]
    cols = mesh.shape[col_axis]

    def shards(embeddings, block_cluster, partner_shift):
        rows, width = embeddings.shape
        vmem = pl.BlockSpec(memory_space=pltpu.VMEM)
        hbm = pl.BlockSpec(memory_space=pl.ANY)
        grad, loss = pl.pallas_call(
            functools.partial(kernel, row_axis, col_axis, devices, cols, width ** (-0.5)),
            out_shape=(
                jax.ShapeDtypeStruct((rows, width), F32),
                jax.ShapeDtypeStruct((rows,), F32),
            ),
            in_specs=[hbm, hbm, hbm],
            out_specs=(vmem, vmem),
            scratch_shapes=[
                pltpu.VMEM((24, BLOCK, width), jnp.bfloat16),
                pltpu.VMEM((2 * HALF, width), jnp.bfloat16),
                pltpu.VMEM((16, rows, BLOCK), F32),
                pltpu.VMEM((rows, MOST * BLOCK), F32),
                pltpu.VMEM((rows, MOST * BLOCK), jnp.bfloat16),
                pltpu.VMEM((rows, 1), F32),
                pltpu.VMEM((rows, 1), F32),
                pltpu.VMEM((rows, 1), F32),
                pltpu.VMEM((2, 1, BLOCK), F32),
                pltpu.VMEM((2 * (2 * REACH + 1), 1, BLOCK), F32),
                pltpu.VMEM((rows, 1), F32),
                pltpu.VMEM((rows, 1), jnp.int32),
                pltpu.VMEM((1, rows), jnp.int32),
                pltpu.SMEM(block_cluster.shape, jnp.int32),
                pltpu.VMEM((1, rows), jnp.int32),
                pltpu.SemaphoreType.DMA((96,)),
                pltpu.SemaphoreType.DMA((2,)),
                pltpu.SemaphoreType.DMA((12,)),
                pltpu.SemaphoreType.DMA((12,)),
                pltpu.SemaphoreType.DMA((8,)),
                pltpu.SemaphoreType.DMA((2,)),
                pltpu.SemaphoreType.DMA((40,)),
                pltpu.SemaphoreType.DMA((2 * REACH + 1,)),
                pltpu.SemaphoreType.DMA((2 * REACH + 1,)),
                pltpu.SemaphoreType.DMA((4,)),
            ],
            compiler_params=pltpu.CompilerParams(
                collective_id=0, has_side_effects=True, vmem_limit_bytes=36 * 1024 * 1024
            ),
        )(*[pltpu.with_memory_space_constraint(a, pltpu.HBM) for a in (block_cluster, embeddings, partner_shift.reshape(1, rows))])
        return loss, grad

    in_specs = (P((row_axis, col_axis), None), P(), P((row_axis, col_axis)))
    out_specs = (P((row_axis, col_axis)), P((row_axis, col_axis), None))
    return jax.shard_map(shards, mesh=mesh, in_specs=in_specs, out_specs=out_specs, check_vma=False)
```

time: 58.2 us -> 44.1 us (0.76)
  the two profiles are of different devices: /device:TPU:16 before, /device:TPU:0 now
where the time goes in v1:
time: 44.1 us; the launch traced here: 44 us
  Pallas kernels  41.6 us (94%)
  local copies, waits for them, and re-layouts  1.72 us (4%)
  between operations  0.64 us (1%)
    pallas_call x1, Pallas kernels, shards(): pl.pallas_call(functools.partial(kernel, row_axis, col_axis, devices, col...  41.6 us
    unnamed x2, local copies, waits for them, and re-layouts  1.72 us

profile of v1, /device:TPU:0, one launch (start us, length us, event | category | flops | bytes accessed | tf_op | source)
XLA Modules:
  0.0 44.0 jit_solution(2226010978721745810)
XLA Ops:
  0.6 41.6 %shard_map.50 = (f32[512,768]{1,0:T(8,128)S(1)}, f32[512]{0:T(512)S(1)}) custom-call(s32[64]{0:T(128)} %cluster_hbm.1, bf16[512,768]{1,0:T(8,128)(2,1)} %e_hbm.1, s32[1,512]{1,0:T(1,128)} %bitcast.1), custom_call_target="tpu_custom_call" | custom-call | tf_op jit(solution)/shard_map/pallas_call | solution.py:487
  42.3 0.6 %copy.7 = f32[512]{0:T(512)} copy(f32[512]{0:T(512)S(1)} %get-tuple-element.8) | data formatting | bytes 4096
  42.9 1.1 %copy.8 = f32[512,768]{1,0:T(8,128)} copy(f32[512,768]{1,0:T(8,128)S(1)} %get-tuple-element.9) | data formatting | bytes 3145728

commit v2 on v1

--- a/solution.py
+++ b/solution.py
@@ -17,30 +17,41 @@
 MESH = pl.DeviceIdType.MESH
 
 X_IN = (
-    (40, 41, 34, 35, 36, 37, 38, 39, 32, 33, 10, 11),
+    (40, 34, 41, 35, 36, 37, 38, 39, 32, 33, 10, 11),
     (38, 44, 39, 45, 43, 42, 14, 15, 33, 32, 37, 36),
 )
 Y_IN = (
-    (20, 21, 30, 31, 22, 23, 28, 29, 12, 13, 14, 15),
-    (27, 26, 25, 24, 40, 41, 16, 17, 18, 19, 34, 35),
+    (20, 30, 21, 31, 22, 28, 23, 29, 12, 13, 14, 15),
+    (27, 16, 26, 25, 24, 40, 41, 17, 18, 19, 34, 35),
 )
 Z_IN = (
-    (8, 9, 2, 3, 4, 5, 6, 7),
-    (6, 12, 7, 13, 8, 11, 9, 10),
+    (8, 2, 9, 3, 4, 5, 6, 7),
+    (6, 12, 7, 13, 11, 8, 10, 9),
 )
 BACK = ((17, 16), (21, 20))
 OWN = (((16, 17, 18, 19), (24, 25, 26, 27)), ((20, 21, 22, 23), (28, 29, 30, 31)))
-SCORE = (
-    (
-        {0: (12, 13), 2: (10,), 4: (4, 15), 6: (1, 11), 8: (2, 14), 10: (3, 16), 11: (6,), 12: (5, 7)},
-        {0: (8, 9), 2: (20, 10), 4: (17, 15), 6: (18, 11), 8: (19, 14), 10: (16, 6), 12: (5, 7)},
-    ),
-    (
-        {0: (14, 15), 2: (13,), 4: (12,), 5: (3,), 6: (6,), 8: (7, 8), 9: (4,), 10: (5, 9), 11: (16,), 12: (17, 18)},
-        {0: (10, 11), 2: (13,), 3: (19,), 4: (12, 22), 6: (20, 21), 8: (7, 8), 10: (9, 16), 12: (17, 18)},
-    ),
-)
 STEPS = 13
+
+
+def pairs_of(t, k):
+    low = 8 * k + 4 * t + 2
+    ready = [[] for _ in range(STEPS)]
+    for s in OWN[t][1 - k]:
+        ready[0].append(s)
+    for i in range(12):
+        for s in (X_IN[t][i], Y_IN[t][i]):
+            ready[i + 1].append(s)
+    for i in range(8):
+        ready[i + 3].append(Z_IN[t][i])
+    pool, out = [], []
+    for u in range(STEPS):
+        pool += [s for s in ready[u] if low <= s < low + 32]
+        now = []
+        while len(pool) >= 2 and len(now) < 2:
+            now.append((pool.pop(0), pool.pop(0)))
+        out.append(now)
+    assert not pool and sum(map(len, out)) == 14
+    return out
 
 
 def events_of(t):
@@ -125,13 +136,13 @@
     pl.semaphore_wait(barrier, count)
 
     n = e_hbm.shape[0]
-    first = 8 + 2 * g
+    first = 16 + 4 * g
 
     def slot_of(s):
         return s + x * (47 - 2 * s)
 
     def rows(slot, half):
-        return buf.at[slot // 2, pl.ds(pl.multiple_of(slot % 2 * CHUNK + half * HALF, HALF), HALF), :]
+        return buf.at[slot, pl.ds(pl.multiple_of(half * HALF, HALF), HALF), :]
 
     def copy(src, dst, send, receive, device):
         return pltpu.make_async_remote_copy(
@@ -198,16 +209,12 @@
             return False
         return both(need, z_recv if s < 16 else True)
 
-    def c_all(t):
-        places = [(s, j) for j, s in enumerate(X_IN[t] + Y_IN[t] + Z_IN[t])]
-        return [(s, j, c_cond(t, s)) for s, j in places if c_cond(t, s) is not False]
-
     plans = [events_of(t) for t in range(2)]
 
     own_copies = [
-        pltpu.make_async_copy(e_hbm.at[pl.ds(h * BLOCK, BLOCK), :], buf.at[first + h], own_sem.at[3 * h]) for h in range(2)]
-    cluster_copy = pltpu.make_async_copy(cluster_hbm, cluster_ref, own_sem.at[1])
-    shift_copy = pltpu.make_async_copy(shift_hbm, shift_ref, own_sem.at[2])
+        pltpu.make_async_copy(e_hbm.at[pl.ds(h * CHUNK, CHUNK), :], buf.at[first + h], own_sem.at[2 + h]) for h in range(4)]
+    cluster_copy = pltpu.make_async_copy(cluster_hbm, cluster_ref, own_sem.at[0])
+    shift_copy = pltpu.make_async_copy(shift_hbm, shift_ref, own_sem.at[1])
     for t in range(2):
         for k in range(2):
             @pl.when((yt == t) & (ct == k))
@@ -278,7 +285,7 @@
 
     adj = 32 * x
     when(~z_recv, lambda: buf.__setitem__(
-        pl.ds(adj // 2, 8), jnp.zeros((8, *buf.shape[1:]), buf.dtype)))
+        pl.ds(adj, 16), jnp.zeros((16, *buf.shape[1:]), buf.dtype)))
     for offset in (-4, -3, -2, -1, 1, 2, 3, 4):
         when(~exists(me + offset), lambda: lse_far.__setitem__(
             pl.ds(2 * (offset + REACH), 2), jnp.zeros((2, *lse_far.shape[1:]), F32)))
@@ -307,37 +314,41 @@
     own_scores = []
     for h in range(2):
         s = lax.dot_general(
-            buf[pl.ds(first, 2)].reshape(n, -1), buf[first + h], (((1,), (1,)), ((), ())),
+            buf[pl.ds(first, 4)].reshape(n, -1), buf[pl.ds(first + 2 * h, 2)].reshape(BLOCK, -1), (((1,), (1,)), ((), ())),
             preferred_element_type=F32) * scale
         cell = lane + h * BLOCK
         hit = jnp.sum(jnp.where(q == cell, s, 0.0), axis=1, keepdims=True)
         own_scores.append(hit)
         ok = jnp.concatenate(
             [jnp.full((BLOCK, BLOCK), alive(7 + h, r).astype(jnp.int32), jnp.int32) for r in range(2)], 0) > 0
-        scores[7 + h] = jnp.where(ok & (half != cell), s, NEG)
+        s = jnp.where(ok & (half != cell), s, NEG)
+        for i in range(2):
+            scores[14 + 2 * h + i] = s[:, i * CHUNK:(i + 1) * CHUNK]
     pos_score[...] = own_scores[0] + own_scores[1]
-    m = jnp.maximum(jnp.max(scores[7], axis=1, keepdims=True), jnp.max(scores[8], axis=1, keepdims=True))
+    near = [scores[14 + i] for i in range(4)]
+    m = functools.reduce(jnp.maximum, near)
     top[...] = m
-    total[...] = jnp.sum(jnp.exp(scores[7] - m), axis=1, keepdims=True) + jnp.sum(
-        jnp.exp(scores[8] - m), axis=1, keepdims=True)
-
-    def process(block):
-        k = block - (2 * g + 1)
-
-        @pl.when((k >= 0) & (k < 16))
+    total[...] = functools.reduce(jnp.add, [jnp.exp(s - m) for s in near])
+
+    def process(slots):
+        ks = [slot // 2 - (2 * g + 1) for slot in slots]
+
+        @pl.when(slots[0] >= 0)
         def _():
-            far = buf[block]
+            far = jnp.concatenate([buf[slot] for slot in slots], 0)
+            s = lax.dot_general(
+                buf[pl.ds(first, 4)].reshape(n, -1), far,
+                (((1,), (1,)), ((), ())), preferred_element_type=F32) * scale
             for r in range(2):
-                part = pl.ds(r * BLOCK, BLOCK)
-                s = lax.dot_general(
-                    buf[first + r], far,
-                    (((1,), (1,)), ((), ())), preferred_element_type=F32) * scale
-                s = jnp.where(alive(k, r), s, NEG)
-                scores[k, part, :] = s
+                part = slice(r * BLOCK, (r + 1) * BLOCK)
+                halves = [
+                    jnp.where(alive(k, r), s[part, i * CHUNK:(i + 1) * CHUNK], NEG) for i, k in enumerate(ks)]
+                for slot, value in zip(slots, halves):
+                    scores[slot - (4 * g + 2), part, :] = value
                 old = top[part, :]
-                new = jnp.maximum(old, jnp.max(s, axis=1, keepdims=True))
-                total[part, :] = total[part, :] * jnp.exp(old - new) + jnp.sum(
-                    jnp.exp(s - new), axis=1, keepdims=True)
+                new = jnp.maximum(old, jnp.maximum(*halves))
+                total[part, :] = total[part, :] * jnp.exp(old - new) + (
+                    jnp.exp(halves[0] - new) + jnp.exp(halves[1] - new))
                 top[part, :] = new
 
     def event(t, kind, i, sends):
@@ -360,46 +371,69 @@
                     when(need, lambda: c_copy(s, j).start())
         run()
 
-    def step(u, carry):
-        spots = [jnp.int32(-1), jnp.int32(-1)]
-        for index in range(STEPS):
+    pairs = [[pairs_of(t, k) for k in range(2)] for t in range(2)]
+
+    def spent(t, u):
+        lists, first_sends, steps = plans[t]
+        started = {item: -1 for item in first_sends}
+        started.update({item: v for v, events in enumerate(steps) for _, _, sends in events for item in sends})
+        for (link, i), v in started.items():
+            due = min(max(i, v) + 3 if link != "Z" else v + 4, STEPS)
+            if due == u:
+                when(link_cond(t, link, i), lambda: link_copy(t, lists, link, i, False).wait_send())
+        for v, events in enumerate(steps):
+            if min(v + 2, STEPS) == u:
+                for kind, i, _ in events:
+                    if kind != "T":
+                        s = {"X": X_IN, "Y": Y_IN, "Z": Z_IN}[kind][t][i]
+                        need = c_cond(t, s)
+                        if need is not False:
+                            when(need, lambda: c_copy(s, i + {"X": 0, "Y": 12, "Z": 24}[kind]).wait_send())
+        if u == 3:
+            for i in range(2):
+                when(z_recv, lambda: back_copy(t, i, False).wait_send())
+            for j in range(8):
+                copy(rows(16, 0), rows(16, 0), cs.at[32 + j], recv.at[0], cpeer).wait_send()
+
+    for u in range(STEPS):
+        for t in range(2):
+            @pl.when(yt == t)
+            def _():
+                for kind, i, sends in plans[t][2][u]:
+                    event(t, kind, i, sends)
+                spent(t, u)
+                for k in range(2):
+                    now = pairs[t][k][u]
+                    if now:
+                        @pl.when(ct == k)
+                        def _():
+                            for s in [s for pair in now for s in pair]:
+                                when(z_recv if s < 16 else True, lambda: arrived(slot_of(s), 1 - c))
+        for h in range(max(len(pairs[t][k][u]) for t in range(2) for k in range(2))):
+            spots = [jnp.int32(-1), jnp.int32(-1)]
             for t in range(2):
                 for k in range(2):
-                    here = (u == index) & (yt == t) & (ct == k)
-                    for h, block in enumerate(SCORE[t][k].get(index, ())):
-                        spots[h] = jnp.where(here, block + x * (23 - 2 * block), spots[h])
-                here = (u == index) & (yt == t)
-
-                @pl.when(here)
-                def _():
-                    for kind, i, sends in plans[t][2][index]:
-                        event(t, kind, i, sends)
-                    for k in range(2):
-                        blocks_now = SCORE[t][k].get(index, ())
-                        if blocks_now:
-                            @pl.when(ct == k)
-                            def _():
-                                for block in blocks_now:
-                                    for s in (2 * block, 2 * block + 1):
-                                        when(z_recv if s < 16 else True, lambda: arrived(slot_of(s), 1 - c))
-        for h in range(2):
-            process(spots[h])
-        return carry
-
-    lax.fori_loop(0, STEPS, step, 0)
-
-    lse = top[...] + jnp.log(total[...])
-    lse_col[...] = lse
-    loss = lse - pos_score[...]
-    pair = jnp.where(
-        lax.broadcasted_iota(jnp.int32, (n, 128), 1) < 8,
-        jnp.broadcast_to(lse, (n, 128)), jnp.broadcast_to(loss, (n, 128)))
-    turned = pair.T
+                    if h < len(pairs[t][k][u]):
+                        here = (yt == t) & (ct == k)
+                        spots = [jnp.where(here, slot_of(s), spot) for s, spot in zip(pairs[t][k][u][h], spots)]
+            process(spots)
+
+    eye = lax.broadcasted_iota(jnp.int32, (CHUNK, CHUNK), 0) == lax.broadcasted_iota(jnp.int32, (CHUNK, CHUNK), 1)
+
+    def as_row(column):
+        return jnp.sum(jnp.where(eye, jnp.broadcast_to(column, (CHUNK, CHUNK)), 0.0), axis=0, keepdims=True)
+
+    lse_rows = []
+    for i in range(n // CHUNK):
+        part = slice(i * CHUNK, (i + 1) * CHUNK)
+        m = jnp.max(top[part, :], axis=1, keepdims=True)
+        t = jnp.sum(total[part, :] * jnp.exp(top[part, :] - m), axis=1, keepdims=True)
+        lse_rows.append(as_row(m) + jnp.log(as_row(t)))
+        lse_col[part, :] = m + jnp.log(t)
     for h in range(2):
-        row = turned[:1, h * BLOCK:(h + 1) * BLOCK]
+        row = jnp.concatenate(lse_rows[2 * h:2 * h + 2], 1)
         lse_send[h] = row
         lse_far[2 * REACH + h] = row
-    loss_ref[...] = turned[8]
 
     def lse_copy(offset):
         return copy(
@@ -408,6 +442,8 @@
 
     for offset in (-4, 4, -3, 3, -2, 2, -1, 1):
         when(exists(me + offset), lambda: lse_copy(offset).start())
+
+    loss_ref[...] = jnp.concatenate([row - as_row(pos_score[i * CHUNK:(i + 1) * CHUNK, :]) for i, row in enumerate(lse_rows)], 1)[0]
 
     lows = []
     for r in range(2):
@@ -417,44 +453,48 @@
         lows.append(low)
 
     for h in range(2):
-        s = scores[7 + h]
+        s = jnp.concatenate([scores[14 + 2 * h + i] for i in range(2)], 1)
         w = jnp.exp(s - lse_col[...]) + jnp.exp(s - lse_far[2 * REACH + h])
         cell = lax.broadcasted_iota(jnp.int32, (n, BLOCK), 1) + h * BLOCK
         line = lax.broadcasted_iota(jnp.int32, (n, BLOCK), 0)
         w = w - (qcol_ref[...] == cell).astype(F32)
         w = w - (qrow_ref[0:1, h * BLOCK:(h + 1) * BLOCK] == line).astype(F32)
         weights[:, h * BLOCK:(h + 1) * BLOCK] = w.astype(jnp.bfloat16)
-        scores[7 + h] = jnp.full((n, BLOCK), NEG, F32)
+        for i in range(2):
+            scores[14 + 2 * h + i] = jnp.full((n, CHUNK), NEG, F32)
 
     width = e_hbm.shape[1]
 
     def own_product(t, carry):
         columns = pl.ds(pl.multiple_of(t * 256, 256), 256)
         grad_ref[:, columns] = jnp.dot(
-            weights[:, :2 * BLOCK], buf[pl.ds(first, 2), :, columns].reshape(n, -1), preferred_element_type=F32)
+            weights[:, :2 * BLOCK], buf[pl.ds(first, 4), :, columns].reshape(n, -1), preferred_element_type=F32)
         return carry
 
     lax.fori_loop(0, width // 256, own_product, 0)
 
     for r in range(2):
         part = pl.ds(r * BLOCK, BLOCK)
-        for j in range(MOST):
-            first_exp[part, j * BLOCK:(j + 1) * BLOCK] = jnp.exp(scores[lows[r] + j, part, :] - lse_col[part, :])
+        for j in range(2 * MOST):
+            first_exp[part, j * CHUNK:(j + 1) * CHUNK] = jnp.exp(scores[2 * lows[r] + j, part, :] - lse_col[part, :])
 
     for offset in (-1, 1, -2, 2, -3, 3, -4, 4):
         when(exists(me + offset), lambda: lse_copy(-offset).wait_recv())
     for r in range(2):
         part = pl.ds(r * BLOCK, BLOCK)
         for j in range(MOST):
-            k = lows[r] + j
-            w = first_exp[part, j * BLOCK:(j + 1) * BLOCK] + jnp.exp(scores[k, part, :] - lse_far[k + 1])
-            weights[part, j * BLOCK:(j + 1) * BLOCK] = w.astype(jnp.bfloat16)
+            far = lse_far[lows[r] + j + 1]
+            for i in range(2):
+                spot = slice((2 * j + i) * CHUNK, (2 * j + i + 1) * CHUNK)
+                w = first_exp[part, spot] + jnp.exp(
+                    scores[2 * lows[r] + 2 * j + i, part, :] - far[:, i * CHUNK:(i + 1) * CHUNK])
+                weights[part, spot] = w.astype(jnp.bfloat16)
 
     for t in range(width // 256):
         columns = pl.ds(t * 256, 256)
         for r in range(2):
             part = pl.ds(r * BLOCK, BLOCK)
-            near = jnp.concatenate([buf[2 * g + 1 + lows[r] + j, :, columns] for j in range(MOST)], 0)
+            near = jnp.concatenate([buf[4 * g + 2 + 2 * lows[r] + j, :, columns] for j in range(2 * MOST)], 0)
             rest = jnp.dot(weights[part, :], near, preferred_element_type=F32)
             grad_ref[part, columns] = (grad_ref[part, columns] + rest) * scale
 
@@ -463,16 +503,7 @@
     for t in range(2):
         @pl.when(yt == t)
         def _():
-            lists = plans[t][0]
-            for link, items in lists.items():
-                for i in range(len(items)):
-                    when(link_cond(t, link, i), lambda: link_copy(t, lists, link, i, False).wait_send())
-            for s, j, need in c_all(t):
-                when(need, lambda: c_copy(s, j).wait_send())
-            for i in range(2):
-                when(z_recv, lambda: back_copy(t, i, False).wait_send())
-    for j in range(8):
-        copy(rows(16, 0), rows(16, 0), cs.at[32 + j], recv.at[0], cpeer).wait_send()
+            spent(t, STEPS)
 
 
 def solution(mesh):
@@ -493,13 +524,13 @@
             in_specs=[hbm, hbm, hbm],
             out_specs=(vmem, vmem),
             scratch_shapes=[
-                pltpu.VMEM((24, BLOCK, width), jnp.bfloat16),
+                pltpu.VMEM((48, CHUNK, width), jnp.bfloat16),
                 pltpu.VMEM((2 * HALF, width), jnp.bfloat16),
-                pltpu.VMEM((16, rows, BLOCK), F32),
+                pltpu.VMEM((32, rows, CHUNK), F32),
                 pltpu.VMEM((rows, MOST * BLOCK), F32),
                 pltpu.VMEM((rows, MOST * BLOCK), jnp.bfloat16),
-                pltpu.VMEM((rows, 1), F32),
-                pltpu.VMEM((rows, 1), F32),
+                pltpu.VMEM((rows, CHUNK), F32),
+                pltpu.VMEM((rows, CHUNK), F32),
                 pltpu.VMEM((rows, 1), F32),
                 pltpu.VMEM((2, 1, BLOCK), F32),
                 pltpu.VMEM((2 * (2 * REACH + 1), 1, BLOCK), F32),
@@ -517,7 +548,7 @@
                 pltpu.SemaphoreType.DMA((40,)),
                 pltpu.SemaphoreType.DMA((2 * REACH + 1,)),
                 pltpu.SemaphoreType.DMA((2 * REACH + 1,)),
-                pltpu.SemaphoreType.DMA((4,)),
+                pltpu.SemaphoreType.DMA((6,)),
             ],
             compiler_params=pltpu.CompilerParams(
                 collective_id=0, has_side_effects=True, vmem_limit_bytes=36 * 1024 * 1024

time: 44.1 us -> 41.8 us (0.948)
  Pallas kernels: 41.6 us -> 39.3 us
    pallas_call x1, Pallas kernels: 41.6 us -> 39.3 us  [shards(): pl.pallas_call(functools.partial(kernel, row_axis, col_axis, devices, col...]
where the time goes in v2:
time: 41.8 us; the launch traced here: 41.6 us
  Pallas kernels  39.3 us (94%)
  local copies, waits for them, and re-layouts  1.72 us (4%)
  between operations  0.64 us (2%)
    pallas_call x1, Pallas kernels, shards(): pl.pallas_call(functools.partial(kernel, row_axis, col_axis, devices, col...  39.3 us
    unnamed x2, local copies, waits for them, and re-layouts  1.72 us

profile of v2, /device:TPU:0, one launch (start us, length us, event | category | flops | bytes accessed | tf_op | source)
XLA Modules:
  0.0 41.6 jit_solution(12947854416720076925)
XLA Ops:
  0.6 39.3 %shard_map.50 = (f32[512,768]{1,0:T(8,128)S(1)}, f32[512]{0:T(512)S(1)}) custom-call(s32[64]{0:T(128)} %cluster_hbm.1, bf16[512,768]{1,0:T(8,128)(2,1)} %e_hbm.1, s32[1,512]{1,0:T(1,128)} %bitcast.1), custom_call_target="tpu_custom_call" | custom-call | tf_op jit(solution)/shard_map/pallas_call | solution.py:518
  39.9 0.6 %copy.7 = f32[512]{0:T(512)} copy(f32[512]{0:T(512)S(1)} %get-tuple-element.8) | data formatting | bytes 4096
  40.5 1.1 %copy.8 = f32[512,768]{1,0:T(8,128)} copy(f32[512,768]{1,0:T(8,128)S(1)} %get-tuple-element.9) | data formatting | bytes 3145728

commit v3 on v2

--- a/solution.py
+++ b/solution.py
@@ -42,7 +42,7 @@
         for s in (X_IN[t][i], Y_IN[t][i]):
             ready[i + 1].append(s)
     for i in range(8):
-        ready[i + 3].append(Z_IN[t][i])
+        ready[i // 2 * 2 + 4].append(Z_IN[t][i])
     pool, out = [], []
     for u in range(STEPS):
         pool += [s for s in ready[u] if low <= s < low + 32]
@@ -76,13 +76,13 @@
         now = []
         if u < 12:
             now += [("X", u, ("S", X_IN[t][u])), ("Y", u, ("S", Y_IN[t][u]))]
-        if u < 2:
-            now.append(("T", u, ("T", u)))
-        if 2 <= u < 10:
-            now.append(("Z", u - 2, ("S", Z_IN[t][u - 2])))
+        if u == 1:
+            now.append(("T", 0, ("T", 0), ("T", 1)))
+        if u in (3, 5, 7, 9):
+            now.append(("Z", (u - 3) // 2, *[("S", s) for s in Z_IN[t][u - 3:u - 1]]))
         done = []
-        for kind, i, item in now:
-            have.add(item)
+        for kind, i, *items in now:
+            have.update(items)
             done.append((kind, i, ready()))
         steps.append(done)
     assert all(ahead[link] == len(items) for link, items in lists.items())
@@ -95,7 +95,7 @@
     grad_ref, loss_ref,
     buf, thru, scores, first_exp, weights, top, total, lse_col, lse_send, lse_far, pos_score, qcol_ref, qrow_ref,
     cluster_ref, shift_ref,
-    recv, trecv, xs, ys, zs, bs, cs, ls, lr, own_sem,
+    rx, ry, rz, rt, rc, ro, sent, ls, lr, own_sem,
 ):
     me = lax.axis_index(row_axis) * cols + lax.axis_index(col_axis)
     y = me % 2
@@ -135,7 +135,7 @@
         count = count + (1 if there is True else there.astype(jnp.int32))
     pl.semaphore_wait(barrier, count)
 
-    n = e_hbm.shape[0]
+    n = e_hbm.shape[0] * CHUNK
     first = 16 + 4 * g
 
     def slot_of(s):
@@ -150,69 +150,67 @@
             device_id=at(device), device_id_type=MESH,
         )
 
-    def arrived(slot, half):
-        copy(rows(slot, half), rows(slot, half), cs.at[0], recv.at[2 * slot + half], cpeer).wait_recv()
-
-    def mine(s):
-        return e_hbm.at[pl.ds(pl.multiple_of((slot_of(s) - 16 - 4 * g) * CHUNK + c * HALF, HALF), HALF), :]
-
-    def source(t, item, own=False):
+    def some(count):
+        return buf.at[pl.ds(0, count), pl.ds(0, HALF), :]
+
+    def got(sem, count):
+        copy(some(count), some(count), sent.at[0], sem, cpeer).wait_recv()
+
+    def gone(sem, count):
+        if count:
+            copy(some(count), some(count), sem, rt.at[0], cpeer).wait_send()
+
+    def mine(s, half):
+        return e_hbm.at[slot_of(s) - first, pl.ds(pl.multiple_of(half * HALF, HALF), HALF), :]
+
+    def source(item, own):
         kind, s = item
         if kind == "T":
             return thru.at[pl.ds(s * HALF, HALF), :]
-        return mine(s) if own else rows(slot_of(s), c)
-
-    def link_copy(t, lists, link, i, own=False):
-        item = lists[link][i]
-        src = source(t, item, own)
+        return mine(s, c) if own else rows(slot_of(s), c)
+
+    def link_cond(t, link, i):
+        if link in "BZ":
+            return "R" if link == "B" else "S"
         if link == "X":
+            return "S" if X_IN[1 - t][i] < 16 else True
+        return "R" if Y_IN[1 - t][i] < 16 else True
+
+    def holds(cond):
+        return {"S": z_send, "R": z_recv, True: True}[cond]
+
+    def link_send(t, lists, link, i, own=False):
+        cond = link_cond(t, link, i)
+        sem = sent.at[{True: 0, "S": 1, "R": 2}[cond]]
+        if link == "B":
+            todo = copy(source(("S", BACK[t][i]), own), thru.at[pl.ds(i * HALF, HALF), :], sem, rt.at[0], zfrom)
+        elif link == "X":
             s = X_IN[1 - t][i]
-            slot = s + (1 - x) * (47 - 2 * s)
-            return copy(src, rows(slot, c), xs.at[i], recv.at[2 * slot + c], xpeer)
-        if link == "Y":
-            slot = slot_of(Y_IN[1 - t][i])
-            return copy(src, rows(slot, c), ys.at[i], recv.at[2 * slot + c], ypeer)
-        slot = slot_of(Z_IN[t][i])
-        return copy(src, rows(slot, c), zs.at[i], recv.at[2 * slot + c], zto)
-
-    def link_cond(t, link, i):
-        if link == "Z":
-            return z_send
-        if link == "X":
-            return z_send if X_IN[1 - t][i] < 16 else True
-        return z_recv if Y_IN[1 - t][i] < 16 else True
-
-    def back_copy(t, i, own=False):
-        src = source(t, ("S", BACK[t][i]), own)
-        return copy(src, thru.at[pl.ds(i * HALF, HALF), :], bs.at[i], trecv.at[i], zfrom)
-
-    def own_half(i, half):
-        return e_hbm.at[pl.ds(i * CHUNK + half * HALF, HALF), :]
-
-    def c_own(i, half, j):
-        slot = 16 + 4 * g + i
-        return copy(own_half(i, half), rows(slot, half), cs.at[32 + j], recv.at[2 * slot + half], cpeer)
-
-    def c_copy(s, j):
-        slot = slot_of(s)
-        return copy(rows(slot, c), rows(slot, c), cs.at[j], recv.at[2 * slot + c], cpeer)
-
-    def c_cond(t, s):
-        low = [8 * k + 4 * t + 2 <= s <= 8 * k + 4 * t + 33 for k in range(2)]
-        if low[0] and low[1]:
-            need = True
-        elif low[0]:
-            need = ct == 1
-        elif low[1]:
-            need = ct == 0
+            todo = copy(source(lists[link][i], own), rows(s + (1 - x) * (47 - 2 * s), c), sem, rx.at[i], xpeer)
+        elif link == "Y":
+            todo = copy(source(lists[link][i], own), rows(slot_of(Y_IN[1 - t][i]), c), sem, ry.at[i], ypeer)
         else:
-            return False
-        return both(need, z_recv if s < 16 else True)
+            todo = copy(source(lists[link][i], own), rows(slot_of(Z_IN[t][i]), c), sem, rz.at[i // 2], zto)
+        when(holds(cond), lambda: todo.start())
+
+    pairs = [[pairs_of(t, k) for k in range(2)] for t in range(2)]
+
+    def pair_of(t, k, s):
+        return [s in pair for now in pairs[t][k] for pair in now].index(True)
+
+    def c_need(t, s):
+        return [k for k in range(2) if 8 * (1 - k) + 4 * t + 2 <= s <= 8 * (1 - k) + 4 * t + 33]
+
+    def c_send(t, s):
+        for k in c_need(t, s):
+            sem = sent.at[2 if s < 16 else 3]
+            spot = rows(slot_of(s), c)
+            when(both(ct == k, z_recv if s < 16 else True), lambda: copy(
+                spot, spot, sem, rc.at[pair_of(t, 1 - k, s)], cpeer).start())
 
     plans = [events_of(t) for t in range(2)]
 
-    own_copies = [
-        pltpu.make_async_copy(e_hbm.at[pl.ds(h * CHUNK, CHUNK), :], buf.at[first + h], own_sem.at[2 + h]) for h in range(4)]
+    own_copy = pltpu.make_async_copy(e_hbm, buf.at[pl.ds(first, 4)], own_sem.at[2])
     cluster_copy = pltpu.make_async_copy(cluster_hbm, cluster_ref, own_sem.at[0])
     shift_copy = pltpu.make_async_copy(shift_hbm, shift_ref, own_sem.at[1])
     for t in range(2):
@@ -226,12 +224,8 @@
                     return BACK[t][i] if link == "B" else lists[link][i][1]
 
                 def send(link, i, own):
-                    if link == "B":
-                        when(z_recv, lambda: back_copy(t, i, own).start())
-                    else:
-                        when(link_cond(t, link, i), lambda: link_copy(t, lists, link, i, own).start())
-
-                started = {"X": 0, "Y": 0, "B": 0}
+                    link_send(t, lists, link, i, own)
+
                 queue = {link: [i for name, i in opening if name == link] for link in ("X", "Y", "B")}
                 plan = {}
                 for link, items in queue.items():
@@ -256,19 +250,18 @@
                 for s in [s for link, i in [*leads, *uses] for s in [slot_at(link, i)]] + list(OWN[t][k]):
                     if s in OWN[t][k] and s not in order:
                         order.append(s)
-                for j, s in enumerate(order):
-                    i = slot_of(s) - 16 - 4 * g
+                for s in order:
                     copy(
-                        e_hbm.at[pl.ds(pl.multiple_of(i * CHUNK + (1 - c) * HALF, HALF), HALF), :],
-                        rows(slot_of(s), 1 - c), cs.at[32 + j], recv.at[2 * slot_of(s) + 1 - c], cpeer).start()
+                        mine(s, 1 - c), rows(slot_of(s), 1 - c), sent.at[3], ro.at[OWN[t][k].index(s)],
+                        cpeer).start()
                 for link, i in leads[2:]:
                     send(link, i, True)
-                for own_copy in own_copies:
-                    own_copy.start()
+                own_copy.start()
                 cluster_copy.start()
                 shift_copy.start()
-                for j, s in enumerate(order):
-                    copy(mine(s), rows(slot_of(s), c), cs.at[36 + j], recv.at[2 * slot_of(s) + c], cpeer).start()
+                for s in order:
+                    copy(
+                        mine(s, c), rows(slot_of(s), c), sent.at[3], rc.at[pair_of(t, 1 - k, s)], cpeer).start()
                 waited = set()
                 for link, i in uses:
                     s = slot_at(link, i)
@@ -277,11 +270,11 @@
                         continue
                     if s not in waited:
                         waited.add(s)
-                        arrived(slot_of(s), c)
+                        got(ro.at[OWN[t][1 - k].index(s)], 1)
                     send(link, i, False)
                 for s in OWN[t][1 - k]:
                     if s not in waited:
-                        arrived(slot_of(s), c)
+                        got(ro.at[OWN[t][1 - k].index(s)], 1)
 
     adj = 32 * x
     when(~z_recv, lambda: buf.__setitem__(
@@ -306,8 +299,7 @@
     qrow_ref[...] = goal
     qcol_ref[...] = jnp.broadcast_to(goal.astype(F32), (128, n)).T[:, :1].astype(jnp.int32)
 
-    for own_copy in own_copies:
-        own_copy.wait()
+    own_copy.wait()
     half = lax.broadcasted_iota(jnp.int32, (n, BLOCK), 0)
     lane = lax.broadcasted_iota(jnp.int32, (n, BLOCK), 1)
     q = qcol_ref[...]
@@ -353,47 +345,30 @@
 
     def event(t, kind, i, sends):
         lists = plans[t][0]
-
-        def run():
-            if kind == "T":
-                when(z_send, lambda: copy(
-                    thru.at[pl.ds(i * HALF, HALF), :], thru.at[pl.ds(i * HALF, HALF), :],
-                    bs.at[i], trecv.at[i], zto).wait_recv())
-            else:
-                s = {"X": X_IN, "Y": Y_IN, "Z": Z_IN}[kind][t][i]
-                when(z_recv if s < 16 else True, lambda: arrived(slot_of(s), c))
-            for link, j in sends:
-                when(link_cond(t, link, j), lambda: link_copy(t, lists, link, j, False).start())
-            if kind != "T":
-                need = c_cond(t, s)
-                if need is not False:
-                    j = i + {"X": 0, "Y": 12, "Z": 24}[kind]
-                    when(need, lambda: c_copy(s, j).start())
-        run()
-
-    pairs = [[pairs_of(t, k) for k in range(2)] for t in range(2)]
-
-    def spent(t, u):
-        lists, first_sends, steps = plans[t]
-        started = {item: -1 for item in first_sends}
-        started.update({item: v for v, events in enumerate(steps) for _, _, sends in events for item in sends})
-        for (link, i), v in started.items():
-            due = min(max(i, v) + 3 if link != "Z" else v + 4, STEPS)
-            if due == u:
-                when(link_cond(t, link, i), lambda: link_copy(t, lists, link, i, False).wait_send())
-        for v, events in enumerate(steps):
-            if min(v + 2, STEPS) == u:
-                for kind, i, _ in events:
-                    if kind != "T":
-                        s = {"X": X_IN, "Y": Y_IN, "Z": Z_IN}[kind][t][i]
-                        need = c_cond(t, s)
-                        if need is not False:
-                            when(need, lambda: c_copy(s, i + {"X": 0, "Y": 12, "Z": 24}[kind]).wait_send())
-        if u == 3:
-            for i in range(2):
-                when(z_recv, lambda: back_copy(t, i, False).wait_send())
-            for j in range(8):
-                copy(rows(16, 0), rows(16, 0), cs.at[32 + j], recv.at[0], cpeer).wait_send()
+        if kind == "T":
+            when(z_send, lambda: got(rt.at[0], 2))
+            slots = []
+        elif kind == "Z":
+            when(z_recv, lambda: got(rz.at[i], 2))
+            slots = Z_IN[t][2 * i:2 * i + 2]
+        else:
+            slots = [{"X": X_IN, "Y": Y_IN}[kind][t][i]]
+            sem = {"X": rx, "Y": ry}[kind].at[i]
+            when(z_recv if slots[0] < 16 else True, lambda: got(sem, 1))
+        for link, j in sends:
+            link_send(t, lists, link, j)
+        for s in slots:
+            c_send(t, s)
+
+    def c_wait(t, k, pair):
+        sem = rc.at[pair_of(t, k, pair[0])]
+        count = sum(s >= 16 for s in pair)
+        if count == 2:
+            got(sem, 2)
+            return
+        when(z_recv, lambda: got(sem, 2))
+        if count:
+            when(~z_recv, lambda: got(sem, 1))
 
     for u in range(STEPS):
         for t in range(2):
@@ -401,14 +376,13 @@
             def _():
                 for kind, i, sends in plans[t][2][u]:
                     event(t, kind, i, sends)
-                spent(t, u)
                 for k in range(2):
                     now = pairs[t][k][u]
                     if now:
                         @pl.when(ct == k)
                         def _():
-                            for s in [s for pair in now for s in pair]:
-                                when(z_recv if s < 16 else True, lambda: arrived(slot_of(s), 1 - c))
+                            for pair in now:
+                                c_wait(t, k, pair)
         for h in range(max(len(pairs[t][k][u]) for t in range(2) for k in range(2))):
             spots = [jnp.int32(-1), jnp.int32(-1)]
             for t in range(2):
@@ -437,8 +411,7 @@
 
     def lse_copy(offset):
         return copy(
-            lse_send, lse_far.at[pl.ds(2 * (REACH - offset), 2)], ls.at[REACH + offset], lr.at[REACH - offset],
-            me + offset)
+            lse_send, lse_far.at[pl.ds(2 * (REACH - offset), 2)], ls.at[0], lr.at[0], me + offset)
 
     for offset in (-4, 4, -3, 3, -2, 2, -1, 1):
         when(exists(me + offset), lambda: lse_copy(offset).start())
@@ -463,7 +436,7 @@
         for i in range(2):
             scores[14 + 2 * h + i] = jnp.full((n, CHUNK), NEG, F32)
 
-    width = e_hbm.shape[1]
+    width = e_hbm.shape[2]
 
     def own_product(t, carry):
         columns = pl.ds(pl.multiple_of(t * 256, 256), 256)
@@ -478,8 +451,14 @@
         for j in range(2 * MOST):
             first_exp[part, j * CHUNK:(j + 1) * CHUNK] = jnp.exp(scores[2 * lows[r] + j, part, :] - lse_col[part, :])
 
-    for offset in (-1, 1, -2, 2, -3, 3, -4, 4):
-        when(exists(me + offset), lambda: lse_copy(-offset).wait_recv())
+    partners = jnp.minimum(me, REACH) + jnp.minimum(devices - 1 - me, REACH)
+
+    def lse_all(count):
+        spot = lse_far.at[pl.ds(0, 2 * count)]
+        return copy(spot, spot, ls.at[0], lr.at[0], cpeer)
+
+    for count in range(REACH, 2 * REACH + 1):
+        when(partners == count, lambda: lse_all(count).wait_recv())
     for r in range(2):
         part = pl.ds(r * BLOCK, BLOCK)
         for j in range(MOST):
@@ -498,12 +477,19 @@
             rest = jnp.dot(weights[part, :], near, preferred_element_type=F32)
             grad_ref[part, columns] = (grad_ref[part, columns] + rest) * scale
 
-    for offset in (-4, 4, -3, 3, -2, 2, -1, 1):
-        when(exists(me + offset), lambda: lse_copy(offset).wait_send())
+    for count in range(REACH, 2 * REACH + 1):
+        when(partners == count, lambda: lse_all(count).wait_send())
     for t in range(2):
-        @pl.when(yt == t)
-        def _():
-            spent(t, STEPS)
+        conds = [link_cond(t, link, i) for link, items in plans[t][0].items() for i in range(len(items))] + ["R", "R"]
+        arrivals = [s for steps in (X_IN[t], Y_IN[t], Z_IN[t]) for s in steps]
+        for k in range(2):
+            @pl.when((yt == t) & (ct == k))
+            def _():
+                relayed = [s for s in arrivals if k in c_need(t, s)]
+                gone(sent.at[0], conds.count(True))
+                when(z_send, lambda: gone(sent.at[1], conds.count("S")))
+                when(z_recv, lambda: gone(sent.at[2], conds.count("R") + sum(s < 16 for s in relayed)))
+                gone(sent.at[3], 8 + sum(s >= 16 for s in relayed))
 
 
 def solution(mesh):
@@ -539,21 +525,22 @@
                 pltpu.VMEM((1, rows), jnp.int32),
                 pltpu.SMEM(block_cluster.shape, jnp.int32),
                 pltpu.VMEM((1, rows), jnp.int32),
-                pltpu.SemaphoreType.DMA((96,)),
-                pltpu.SemaphoreType.DMA((2,)),
                 pltpu.SemaphoreType.DMA((12,)),
                 pltpu.SemaphoreType.DMA((12,)),
-                pltpu.SemaphoreType.DMA((8,)),
-                pltpu.SemaphoreType.DMA((2,)),
-                pltpu.SemaphoreType.DMA((40,)),
-                pltpu.SemaphoreType.DMA((2 * REACH + 1,)),
-                pltpu.SemaphoreType.DMA((2 * REACH + 1,)),
-                pltpu.SemaphoreType.DMA((6,)),
+                pltpu.SemaphoreType.DMA((4,)),
+                pltpu.SemaphoreType.DMA((1,)),
+                pltpu.SemaphoreType.DMA((14,)),
+                pltpu.SemaphoreType.DMA((4,)),
+                pltpu.SemaphoreType.DMA((4,)),
+                pltpu.SemaphoreType.DMA((1,)),
+                pltpu.SemaphoreType.DMA((1,)),
+                pltpu.SemaphoreType.DMA((3,)),
             ],
             compiler_params=pltpu.CompilerParams(
                 collective_id=0, has_side_effects=True, vmem_limit_bytes=36 * 1024 * 1024
             ),
-        )(*[pltpu.with_memory_space_constraint(a, pltpu.HBM) for a in (block_cluster, embeddings, partner_shift.reshape(1, rows))])
+        )(*[pltpu.with_memory_space_constraint(a, pltpu.HBM) for a in (
+            block_cluster, embeddings.reshape(rows // CHUNK, CHUNK, width), partner_shift.reshape(1, rows))])
         return loss, grad
 
     in_specs = (P((row_axis, col_axis), None), P(), P((row_axis, col_axis)))

time: 41.8 us -> 40.6 us (0.971)
  Pallas kernels: 39.3 us -> 38 us
    pallas_call x1, Pallas kernels: 39.3 us -> 38 us  [shards(): pl.pallas_call(functools.partial(kernel, row_axis, col_axis, devices, col...]
where the time goes in v3:
time: 40.6 us; the launch traced here: 40.4 us
  Pallas kernels  38 us (94%)
  local copies, waits for them, and re-layouts  1.72 us (4%)
  between operations  0.64 us (2%)
    pallas_call x1, Pallas kernels, shards(): pl.pallas_call(functools.partial(kernel, row_axis, col_axis, devices, col...  38 us
    unnamed x2, local copies, waits for them, and re-layouts  1.72 us

profile of v3, /device:TPU:0, one launch (start us, length us, event | category | flops | bytes accessed | tf_op | source)
XLA Modules:
  0.0 40.4 jit_solution(17436074813253891857)
XLA Ops:
  0.6 38.0 %shard_map.50 = (f32[512,768]{1,0:T(8,128)S(1)}, f32[512]{0:T(512)S(1)}) custom-call(s32[64]{0:T(128)} %cluster_hbm.1, bf16[4,128,768]{2,1,0:T(8,128)(2,1)} %bitcast.2, s32[1,512]{1,0:T(1,128)} %bitcast.3), custom_call_target="tpu_custom_call" | custom-call | tf_op jit(solution)/shard_map/pallas_call | solution.py:504
  38.7 0.6 %copy.7 = f32[512]{0:T(512)} copy(f32[512]{0:T(512)S(1)} %get-tuple-element.8) | data formatting | bytes 4096
  39.3 1.1 %copy.8 = f32[512,768]{1,0:T(8,128)} copy(f32[512,768]{1,0:T(8,128)S(1)} %get-tuple-element.9) | data formatting | bytes 3145728

commit v4 on v3

--- a/solution.py
+++ b/solution.py
@@ -492,6 +492,19 @@
                 gone(sent.at[3], 8 + sum(s >= 16 for s in relayed))
 
 
+def store(grad_ref, loss_ref, grad_out, loss_out, sem):
+    parts = 4
+    rows = grad_ref.shape[0] // parts
+    copies = [pltpu.make_async_copy(loss_ref, loss_out, sem.at[parts])]
+    for i in range(parts):
+        spot = (pl.ds(i * rows, rows), slice(None))
+        copies.append(pltpu.make_async_copy(grad_ref.at[spot], grad_out.at[spot], sem.at[i]))
+    for todo in copies:
+        todo.start()
+    for todo in copies:
+        todo.wait()
+
+
 def solution(mesh):
     row_axis, col_axis = mesh.axis_names
     devices = mesh.shape[row_axis] * mesh.shape[col_axis]
@@ -541,6 +554,14 @@
             ),
         )(*[pltpu.with_memory_space_constraint(a, pltpu.HBM) for a in (
             block_cluster, embeddings.reshape(rows // CHUNK, CHUNK, width), partner_shift.reshape(1, rows))])
+        grad, loss = pl.pallas_call(
+            store,
+            out_shape=(jax.ShapeDtypeStruct(grad.shape, F32), jax.ShapeDtypeStruct(loss.shape, F32)),
+            in_specs=[vmem, vmem],
+            out_specs=(hbm, hbm),
+            scratch_shapes=[pltpu.SemaphoreType.DMA((5,))],
+            compiler_params=pltpu.CompilerParams(vmem_limit_bytes=36 * 1024 * 1024),
+        )(grad, loss)
         return loss, grad
 
     in_specs = (P((row_axis, col_axis), None), P(), P((row_axis, col_axis)))

time: 40.6 us -> 40.2 us (level)
  local copies, waits for them, and re-layouts: 1.72 us -> 0 us
  Pallas kernels: 38 us -> 39.2 us
    unnamed x2 -> x0, local copies, waits for them, and re-layouts: 1.72 us -> none
    pallas_call x0 -> x1, Pallas kernels: none -> 1.18 us  [shards(): pl.pallas_call(store, out_shape=(jax.ShapeDtypeStruct(grad.shape, F32), j...]
where the time goes in v4:
time: 40.2 us; the launch traced here: 40 us
  Pallas kernels  39.2 us (98%)
  between operations  0.8 us (2%)
    pallas_call x1, Pallas kernels, shards(): pl.pallas_call(functools.partial(kernel, row_axis, col_axis, devices, col...  38 us
    pallas_call x1, Pallas kernels, shards(): pl.pallas_call(store, out_shape=(jax.ShapeDtypeStruct(grad.shape, F32), j...  1.18 us

profile of v4, /device:TPU:0, one launch (start us, length us, event | category | flops | bytes accessed | tf_op | source)
XLA Modules:
  0.0 40.0 jit_solution(421568099865956803)
XLA Ops:
  0.6 38.0 %shard_map.50 = (f32[512,768]{1,0:T(8,128)S(1)}, f32[512]{0:T(512)S(1)}) custom-call(s32[64]{0:T(128)} %cluster_hbm.1, bf16[4,128,768]{2,1,0:T(8,128)(2,1)} %bitcast.2, s32[1,512]{1,0:T(1,128)} %bitcast.3), custom_call_target="tpu_custom_call" | custom-call | tf_op jit(solution)/shard_map/pallas_call | solution.py:517
  38.7 1.2 %shard_map.51 = (f32[512,768]{1,0:T(8,128)}, f32[512]{0:T(512)}) custom-call(f32[512,768]{1,0:T(8,128)S(1)} %get-tuple-element.6.grad_ref, f32[512]{0:T(512)S(1)} %get-tuple-element.7.loss_ref), custom_call_target="tpu_custom_call" | custom-call | tf_op jit(solution)/shard_map/pallas_call | solution.py:557

commit v5 on v4

--- a/solution.py
+++ b/solution.py
@@ -425,6 +425,10 @@
             low = low + jnp.where(alive(k, r), 0, 1)
         lows.append(low)
 
+    def live(r, j):
+        left = jnp.maximum(7 - lows[r], 0)
+        return jnp.where(j < left, lows[r] + j, 9 + j - left)
+
     for h in range(2):
         s = jnp.concatenate([scores[14 + 2 * h + i] for i in range(2)], 1)
         w = jnp.exp(s - lse_col[...]) + jnp.exp(s - lse_far[2 * REACH + h])
@@ -433,8 +437,6 @@
         w = w - (qcol_ref[...] == cell).astype(F32)
         w = w - (qrow_ref[0:1, h * BLOCK:(h + 1) * BLOCK] == line).astype(F32)
         weights[:, h * BLOCK:(h + 1) * BLOCK] = w.astype(jnp.bfloat16)
-        for i in range(2):
-            scores[14 + 2 * h + i] = jnp.full((n, CHUNK), NEG, F32)
 
     width = e_hbm.shape[2]
 
@@ -448,8 +450,10 @@
 
     for r in range(2):
         part = pl.ds(r * BLOCK, BLOCK)
-        for j in range(2 * MOST):
-            first_exp[part, j * CHUNK:(j + 1) * CHUNK] = jnp.exp(scores[2 * lows[r] + j, part, :] - lse_col[part, :])
+        for j in range(MOST - 1):
+            for i in range(2):
+                spot = slice((2 * j + i) * CHUNK, (2 * j + i + 1) * CHUNK)
+                first_exp[part, spot] = jnp.exp(scores[2 * live(r, j) + i, part, :] - lse_col[part, :])
 
     partners = jnp.minimum(me, REACH) + jnp.minimum(devices - 1 - me, REACH)
 
@@ -461,19 +465,20 @@
         when(partners == count, lambda: lse_all(count).wait_recv())
     for r in range(2):
         part = pl.ds(r * BLOCK, BLOCK)
-        for j in range(MOST):
-            far = lse_far[lows[r] + j + 1]
+        for j in range(MOST - 1):
+            far = lse_far[live(r, j) + 1]
             for i in range(2):
                 spot = slice((2 * j + i) * CHUNK, (2 * j + i + 1) * CHUNK)
                 w = first_exp[part, spot] + jnp.exp(
-                    scores[2 * lows[r] + 2 * j + i, part, :] - far[:, i * CHUNK:(i + 1) * CHUNK])
+                    scores[2 * live(r, j) + i, part, :] - far[:, i * CHUNK:(i + 1) * CHUNK])
                 weights[part, spot] = w.astype(jnp.bfloat16)
 
     for t in range(width // 256):
         columns = pl.ds(t * 256, 256)
         for r in range(2):
             part = pl.ds(r * BLOCK, BLOCK)
-            near = jnp.concatenate([buf[4 * g + 2 + 2 * lows[r] + j, :, columns] for j in range(2 * MOST)], 0)
+            near = jnp.concatenate(
+                [buf[4 * g + 2 + 2 * live(r, j) + i, :, columns] for j in range(MOST - 1) for i in range(2)], 0)
             rest = jnp.dot(weights[part, :], near, preferred_element_type=F32)
             grad_ref[part, columns] = (grad_ref[part, columns] + rest) * scale
 
@@ -526,8 +531,8 @@
                 pltpu.VMEM((48, CHUNK, width), jnp.bfloat16),
                 pltpu.VMEM((2 * HALF, width), jnp.bfloat16),
                 pltpu.VMEM((32, rows, CHUNK), F32),
-                pltpu.VMEM((rows, MOST * BLOCK), F32),
-                pltpu.VMEM((rows, MOST * BLOCK), jnp.bfloat16),
+                pltpu.VMEM((rows, (MOST - 1) * BLOCK), F32),
+                pltpu.VMEM((rows, (MOST - 1) * BLOCK), jnp.bfloat16),
                 pltpu.VMEM((rows, CHUNK), F32),
                 pltpu.VMEM((rows, CHUNK), F32),
                 pltpu.VMEM((rows, 1), F32),

time: 40.2 us -> 39.9 us (level)
  no operation moved by 1% of the time
where the time goes in v5:
time: 39.9 us; the launch traced here: 39.8 us
  Pallas kernels  39 us (98%)
  between operations  0.8 us (2%)
    pallas_call x1, Pallas kernels, shards(): pl.pallas_call(functools.partial(kernel, row_axis, col_axis, devices, col...  37.8 us
    pallas_call x1, Pallas kernels, shards(): pl.pallas_call(store, out_shape=(jax.ShapeDtypeStruct(grad.shape, F32), j...  1.18 us

profile of v5, /device:TPU:0, one launch (start us, length us, event | category | flops | bytes accessed | tf_op | source)
XLA Modules:
  0.0 39.8 jit_solution(14808142434631092440)
XLA Ops:
  0.6 37.8 %shard_map.50 = (f32[512,768]{1,0:T(8,128)S(1)}, f32[512]{0:T(512)S(1)}) custom-call(s32[64]{0:T(128)} %cluster_hbm.1, bf16[4,128,768]{2,1,0:T(8,128)(2,1)} %bitcast.2, s32[1,512]{1,0:T(1,128)} %bitcast.3), custom_call_target="tpu_custom_call" | custom-call | tf_op jit(solution)/shard_map/pallas_call | solution.py:522
  38.4 1.2 %shard_map.51 = (f32[512,768]{1,0:T(8,128)}, f32[512]{0:T(512)}) custom-call(f32[512,768]{1,0:T(8,128)S(1)} %get-tuple-element.6.grad_ref, f32[512]{0:T(512)S(1)} %get-tuple-element.7.loss_ref), custom_call_target="tpu_custom_call" | custom-call | tf_op jit(solution)/shard_map/pallas_call | solution.py:562

commit v6 on v5

--- a/solution.py
+++ b/solution.py
@@ -31,6 +31,7 @@
 BACK = ((17, 16), (21, 20))
 OWN = (((16, 17, 18, 19), (24, 25, 26, 27)), ((20, 21, 22, 23), (28, 29, 30, 31)))
 STEPS = 13
+LATE = 8
 
 
 def pairs_of(t, k):
@@ -188,7 +189,7 @@
             s = X_IN[1 - t][i]
             todo = copy(source(lists[link][i], own), rows(s + (1 - x) * (47 - 2 * s), c), sem, rx.at[i], xpeer)
         elif link == "Y":
-            todo = copy(source(lists[link][i], own), rows(slot_of(Y_IN[1 - t][i]), c), sem, ry.at[i], ypeer)
+            todo = copy(source(lists[link][i], own), rows(slot_of(Y_IN[1 - t][i]), c), sem, (ry if i < LATE else rx).at[i], ypeer)
         else:
             todo = copy(source(lists[link][i], own), rows(slot_of(Z_IN[t][i]), c), sem, rz.at[i // 2], zto)
         when(holds(cond), lambda: todo.start())
@@ -353,8 +354,20 @@
             slots = Z_IN[t][2 * i:2 * i + 2]
         else:
             slots = [{"X": X_IN, "Y": Y_IN}[kind][t][i]]
-            sem = {"X": rx, "Y": ry}[kind].at[i]
-            when(z_recv if slots[0] < 16 else True, lambda: got(sem, 1))
+            sem = {"X": rx, "Y": ry}[kind].at[i if kind == "X" or i < LATE else 0]
+            if i < LATE:
+                when(z_recv if slots[0] < 16 else True, lambda: got(sem, 1))
+            elif kind == "X":
+                slots = [X_IN[t][i], Y_IN[t][i]]
+                count = sum(s >= 16 for s in slots)
+                if count == 2:
+                    got(sem, 2)
+                else:
+                    when(z_recv, lambda: got(sem, 2))
+                    if count:
+                        when(~z_recv, lambda: got(sem, 1))
+            else:
+                slots = []
         for link, j in sends:
             link_send(t, lists, link, j)
         for s in slots:
@@ -413,7 +426,7 @@
         return copy(
             lse_send, lse_far.at[pl.ds(2 * (REACH - offset), 2)], ls.at[0], lr.at[0], me + offset)
 
-    for offset in (-4, 4, -3, 3, -2, 2, -1, 1):
+    for offset in (-1, 1, -3, 3, -2, 2, -4, 4):
         when(exists(me + offset), lambda: lse_copy(offset).start())
 
     loss_ref[...] = jnp.concatenate([row - as_row(pos_score[i * CHUNK:(i + 1) * CHUNK, :]) for i, row in enumerate(lse_rows)], 1)[0]
@@ -544,7 +557,7 @@
                 pltpu.SMEM(block_cluster.shape, jnp.int32),
                 pltpu.VMEM((1, rows), jnp.int32),
                 pltpu.SemaphoreType.DMA((12,)),
-                pltpu.SemaphoreType.DMA((12,)),
+                pltpu.SemaphoreType.DMA((LATE,)),
                 pltpu.SemaphoreType.DMA((4,)),
                 pltpu.SemaphoreType.DMA((1,)),
                 pltpu.SemaphoreType.DMA((14,)),

time: 39.9 us -> 40 us (level)
  no operation moved by 1% of the time
where the time goes in v6:
time: 40 us; the launch traced here: 39.9 us
  Pallas kernels  39.1 us (98%)
  between operations  0.8 us (2%)
    pallas_call x1, Pallas kernels, shards(): pl.pallas_call(functools.partial(kernel, row_axis, col_axis, devices, col...  37.9 us
    pallas_call x1, Pallas kernels, shards(): pl.pallas_call(store, out_shape=(jax.ShapeDtypeStruct(grad.shape, F32), j...  1.18 us

profile of v6, /device:TPU:0, one launch (start us, length us, event | category | flops | bytes accessed | tf_op | source)
XLA Modules:
  0.0 39.9 jit_solution(3890489682570624466)
XLA Ops:
  0.6 37.9 %shard_map.50 = (f32[512,768]{1,0:T(8,128)S(1)}, f32[512]{0:T(512)S(1)}) custom-call(s32[64]{0:T(128)} %cluster_hbm.1, bf16[4,128,768]{2,1,0:T(8,128)(2,1)} %bitcast.2, s32[1,512]{1,0:T(1,128)} %bitcast.3), custom_call_target="tpu_custom_call" | custom-call | tf_op jit(solution)/shard_map/pallas_call | solution.py:535
  38.5 1.2 %shard_map.51 = (f32[512,768]{1,0:T(8,128)}, f32[512]{0:T(512)}) custom-call(f32[512,768]{1,0:T(8,128)S(1)} %get-tuple-element.6.grad_ref, f32[512]{0:T(512)S(1)} %get-tuple-element.7.loss_ref), custom_call_target="tpu_custom_call" | custom-call | tf_op jit(solution)/shard_map/pallas_call | solution.py:575

commit v7 on v5

--- a/solution.py
+++ b/solution.py
@@ -413,7 +413,7 @@
         return copy(
             lse_send, lse_far.at[pl.ds(2 * (REACH - offset), 2)], ls.at[0], lr.at[0], me + offset)
 
-    for offset in (-4, 4, -3, 3, -2, 2, -1, 1):
+    for offset in (-1, 1, -3, 3, -2, 2, -4, 4):
         when(exists(me + offset), lambda: lse_copy(offset).start())
 
     loss_ref[...] = jnp.concatenate([row - as_row(pos_score[i * CHUNK:(i + 1) * CHUNK, :]) for i, row in enumerate(lse_rows)], 1)[0]
@@ -498,7 +498,7 @@
 
 
 def store(grad_ref, loss_ref, grad_out, loss_out, sem):
-    parts = 4
+    parts = 1
     rows = grad_ref.shape[0] // parts
     copies = [pltpu.make_async_copy(loss_ref, loss_out, sem.at[parts])]
     for i in range(parts):
@@ -564,7 +564,7 @@
             out_shape=(jax.ShapeDtypeStruct(grad.shape, F32), jax.ShapeDtypeStruct(loss.shape, F32)),
             in_specs=[vmem, vmem],
             out_specs=(hbm, hbm),
-            scratch_shapes=[pltpu.SemaphoreType.DMA((5,))],
+            scratch_shapes=[pltpu.SemaphoreType.DMA((2,))],
             compiler_params=pltpu.CompilerParams(vmem_limit_bytes=36 * 1024 * 1024),
         )(grad, loss)
         return loss, grad

time: 39.9 us -> 40 us (level)
  no operation moved by 1% of the time
where the time goes in v7:
time: 40 us; the launch traced here: 39.8 us
  Pallas kernels  39 us (98%)
  between operations  0.8 us (2%)
    pallas_call x1, Pallas kernels, shards(): pl.pallas_call(functools.partial(kernel, row_axis, col_axis, devices, col...  37.9 us
    pallas_call x1, Pallas kernels, shards(): pl.pallas_call(store, out_shape=(jax.ShapeDtypeStruct(grad.shape, F32), j...  1.17 us

profile of v7, /device:TPU:0, one launch (start us, length us, event | category | flops | bytes accessed | tf_op | source)
XLA Modules:
  0.0 39.8 jit_solution(10943985732054733147)
XLA Ops:
  0.6 37.9 %shard_map.50 = (f32[512,768]{1,0:T(8,128)S(1)}, f32[512]{0:T(512)S(1)}) custom-call(s32[64]{0:T(128)} %cluster_hbm.1, bf16[4,128,768]{2,1,0:T(8,128)(2,1)} %bitcast.2, s32[1,512]{1,0:T(1,128)} %bitcast.3), custom_call_target="tpu_custom_call" | custom-call | tf_op jit(solution)/shard_map/pallas_call | solution.py:522
  38.5 1.2 %shard_map.51 = (f32[512,768]{1,0:T(8,128)}, f32[512]{0:T(512)}) custom-call(f32[512,768]{1,0:T(8,128)S(1)} %get-tuple-element.6.grad_ref, f32[512]{0:T(512)S(1)} %get-tuple-element.7.loss_ref), custom_call_target="tpu_custom_call" | custom-call | tf_op jit(solution)/shard_map/pallas_call | solution.py:562
